TPU v7x, 1024 devices: a whole 8x8x8 slice. The times are simulated.
1024 devices in a mesh: band: 32 (over y, x_hi), grid: 32 (over z, x_lo, core).
Axes of the slice: x: 8 (x_hi: 4, x_lo: 2; x = x_hi * 2 + x_lo), y: 8, z: 8, core: 2. Of those that a mesh axis runs over, the one named last changes fastest.
Arguments:
- orbitals: float32 [5120, 49152], P('band', 'grid'), may hold values from -6 to 6
Outputs:
- corrected: float32 [5120, 49152], P('band', 'grid')
All inputs are finite; a program needn't handle non-finite values.
Results may differ from a plain program's by a relative error of at most 0.0001.
Values sent between devices are 32-bit elements; how exact they have to be, the bound alone decides.
No kernel may reach another device: no remote copies, remote signals or barrier semaphores. Data moves between devices by JAX's collectives and lax.ppermute only.
A program may use at most 32 MiB of HBM per device.

v0:
```python
import jax
import jax.numpy as jnp
from jax import lax
from jax.sharding import PartitionSpec as P


def passed_along(block, axis, distance):
    devices = range(lax.axis_size(axis))
    route = [((i - distance) % len(devices), i) for i in devices]
    return lax.ppermute(block, axis, route)


def product(left, right):
    return jnp.dot(left, right, precision=lax.Precision.HIGHEST, preferred_element_type=jnp.float32)


def shards(orbitals):
    band_count = lax.axis_size("band")
    shifts = min(4, (band_count - 1) // 2)
    points = orbitals.shape[1] * lax.axis_size("grid")
    others = []
    for distance in range(1, shifts + 1):
        others.append(passed_along(orbitals, "band", distance))
    neighbours = [orbitals] + others
    partials = [product(orbitals, other.T) for other in neighbours]
    summed = lax.psum(jnp.stack(partials), "grid") / points
    tiles = [summed[index] for index in range(shifts + 1)]
    identity = jnp.eye(orbitals.shape[0], dtype=jnp.float32)
    fix = product(tiles[0] - identity, orbitals)
    terms = [None]
    for distance in range(1, shifts + 1):
        fix = fix + product(tiles[distance], others[distance - 1])
        terms.append(product(tiles[distance].T, orbitals))
    for distance in range(1, shifts + 1):
        fix = fix + passed_along(terms[distance], "band", -distance)
    return orbitals - 0.5 * fix


def solution(mesh):
    return jax.shard_map(
        shards,
        mesh=mesh,
        in_specs=(P("band", "grid"),),
        out_specs=P("band", "grid"),
        check_vma=False,
    )
```

profile of v0, /device:TPU:1, one launch (start us, length us, event | category | flops | bytes accessed | tf_op | source)
XLA Modules:
  0.0 489.6 jit_solution(6646921365109627468)
XLA Ops:
  6.5 5.0 %collective-permute-start = (f32[160,1536]{1,0:T(8,128)}, f32[160,1536]{1,0:T(8,128)S(1)}, u32[]{:S(2)}, u32[]{:S(2)}) collective-permute-start(f32[160,1536]{1,0:T(8,128)} %param.1), channel_id=1, source_target_pairs={{992,0},{0,32},{32,64},{64,96},{96,128},{128,160},{160,192},{192,2... | collective-permute-start | bytes 2949128 | tf_op jit(solution)/shard_map/ppermute | solution.py:10
  11.5 5.3 %collective-permute-start.1 = (f32[160,1536]{1,0:T(8,128)}, f32[160,1536]{1,0:T(8,128)S(1)}, u32[]{:S(2)}, u32[]{:S(2)}) collective-permute-start(f32[160,1536]{1,0:T(8,128)} %param.1), channel_id=1, source_target_pairs={{960,0},{992,32},{0,64},{32,96},{64,128},{96,160},{128,192},{160,2... | collective-permute-start | bytes 2949128 | tf_op jit(solution)/shard_map/ppermute | solution.py:10
  16.9 6.3 %collective-permute-start.2 = (f32[160,1536]{1,0:T(8,128)}, f32[160,1536]{1,0:T(8,128)S(1)}, u32[]{:S(2)}, u32[]{:S(2)}) collective-permute-start(f32[160,1536]{1,0:T(8,128)} %param.1), channel_id=1, source_target_pairs={{928,0},{960,32},{992,64},{0,96},{32,128},{64,160},{96,192},{128,2... | collective-permute-start | bytes 2949128 | tf_op jit(solution)/shard_map/ppermute | solution.py:10
  23.1 3.3 collective-permute-start.3
  26.5 3.4 fusion.12
  29.8 10.1 %collective-permute-done = f32[160,1536]{1,0:T(8,128)S(1)} collective-permute-done((f32[160,1536]{1,0:T(8,128)}, f32[160,1536]{1,0:T(8,128)S(1)}, u32[]{:S(2)}, u32[]{:S(2)}) %collective-permute-start) | collective-permute-done | bytes 983072 | tf_op jit(solution)/shard_map/ppermute | solution.py:10
  39.9 1.6 fusion.11
  41.6 59.3 %collective-permute-done.1 = f32[160,1536]{1,0:T(8,128)S(1)} collective-permute-done((f32[160,1536]{1,0:T(8,128)}, f32[160,1536]{1,0:T(8,128)S(1)}, u32[]{:S(2)}, u32[]{:S(2)}) %collective-permute-start.1) | collective-permute-done | bytes 983072 | tf_op jit(solution)/shard_map/ppermute | solution.py:10
  100.8 1.6 fusion.10
  102.4 9.6 %collective-permute-done.2 = f32[160,1536]{1,0:T(8,128)S(1)} collective-permute-done((f32[160,1536]{1,0:T(8,128)}, f32[160,1536]{1,0:T(8,128)S(1)}, u32[]{:S(2)}, u32[]{:S(2)}) %collective-permute-start.2) | collective-permute-done | bytes 983072 | tf_op jit(solution)/shard_map/ppermute | solution.py:10
  112.0 1.6 fusion.9
  114.6 1.6 fusion.8
  116.2 246.9 %all-reduce.2.cloned.1.call-done = f32[5,160,160]{2,1,0:T(8,128)} async-done(((f32[5,160,160]{2,1,0:T(8,128)}), f32[5,160,160]{2,1,0:T(8,128)}) %all-reduce.2.cloned.1.call-update) | async-done | bytes 512016 | tf_op jit(solution)/shard_map/psum | solution.py:26
  363.2 1.2 broadcast_multiply_fusion
  364.4 1.0 fusion.21
  365.4 1.0 fusion.19
  366.4 1.0 fusion.18
  367.5 1.0 fusion.17
  368.5 6.8 %collective-permute-start.4 = (f32[160,1536]{1,0:T(8,128)S(1)}, f32[160,1536]{1,0:T(8,128)S(1)}, u32[]{:S(2)}, u32[]{:S(2)}) collective-permute-start(f32[160,1536]{1,0:T(8,128)S(1)} %fusion.17), channel_id=1, source_target_pairs={{32,0},{64,32},{96,64},{128,96},{160,128},{192,160},{224,192},{256... | collective-permute-start | bytes 2949128 | tf_op jit(solution)/shard_map/ppermute | solution.py:10
  375.3 4.8 collective-permute-start.5
  380.1 4.0 collective-permute-start.6
  384.1 3.2 collective-permute-start.7
  391.4 89.0 %collective-permute-done.4 = f32[160,1536]{1,0:T(8,128)S(1)} collective-permute-done((f32[160,1536]{1,0:T(8,128)S(1)}, f32[160,1536]{1,0:T(8,128)S(1)}, u32[]{:S(2)}, u32[]{:S(2)}) %collective-permute-start.4) | collective-permute-done | bytes 983072 | tf_op jit(solution)/shard_map/ppermute | solution.py:10
  480.5 2.3 fusion.7
  (20 shorter events, 5.0 us)
Async XLA Ops:
  6.5 33.4 %copy-start = (f32[160,1536]{1,0:T(8,128)S(1)}, f32[160,1536]{1,0:T(8,128)}, u32[]{:S(2)}) copy-start(f32[160,1536]{1,0:T(8,128)} %param.1) | copy-start | bytes 2949124
  6.5 356.6 %all-reduce.2.cloned.1.call-start = ((), (), s32[]{:S(2)}) async-start(), calls=%async_computation | async-start | bytes 1638400 | tf_op jit(solution)/shard_map/psum | solution.py:26
  6.5 33.4 %collective-permute-start = (f32[160,1536]{1,0:T(8,128)}, f32[160,1536]{1,0:T(8,128)S(1)}, u32[]{:S(2)}, u32[]{:S(2)}) collective-permute-start(f32[160,1536]{1,0:T(8,128)} %param.1), channel_id=1, source_target_pairs={{992,0},{0,32},{32,64},{64,96},{96,128},{128,160},{160,192},{192,2... | collective-permute-start | bytes 2949128 | tf_op jit(solution)/shard_map/ppermute | solution.py:10
  11.5 89.3 %collective-permute-start.1 = (f32[160,1536]{1,0:T(8,128)}, f32[160,1536]{1,0:T(8,128)S(1)}, u32[]{:S(2)}, u32[]{:S(2)}) collective-permute-start(f32[160,1536]{1,0:T(8,128)} %param.1), channel_id=1, source_target_pairs={{960,0},{992,32},{0,64},{32,96},{64,128},{96,160},{128,192},{160,2... | collective-permute-start | bytes 2949128 | tf_op jit(solution)/shard_map/ppermute | solution.py:10
  16.9 95.2 %collective-permute-start.2 = (f32[160,1536]{1,0:T(8,128)}, f32[160,1536]{1,0:T(8,128)S(1)}, u32[]{:S(2)}, u32[]{:S(2)}) collective-permute-start(f32[160,1536]{1,0:T(8,128)} %param.1), channel_id=1, source_target_pairs={{928,0},{960,32},{992,64},{0,96},{32,128},{64,160},{96,192},{128,2... | collective-permute-start | bytes 2949128 | tf_op jit(solution)/shard_map/ppermute | solution.py:10
  23.1 90.5 %collective-permute-start.3 = (f32[160,1536]{1,0:T(8,128)}, f32[160,1536]{1,0:T(8,128)S(1)}, u32[]{:S(2)}, u32[]{:S(2)}) collective-permute-start(f32[160,1536]{1,0:T(8,128)} %param.1), channel_id=1, source_target_pairs={{896,0},{928,32},{960,64},{992,96},{0,128},{32,160},{64,192},{96,2... | collective-permute-start | bytes 2949128 | tf_op jit(solution)/shard_map/ppermute | solution.py:10
  112.0 1.6 copy-start.1
  113.6 0.9 copy-start.3
  368.5 19.8 %copy-start.4 = (f32[160,1536]{1,0:T(8,128)S(1)}, f32[160,1536]{1,0:T(8,128)}, u32[]{:S(2)}) copy-start(f32[160,1536]{1,0:T(8,128)} %copy-done.3) | copy-start | bytes 2949124
  368.5 111.9 %collective-permute-start.4 = (f32[160,1536]{1,0:T(8,128)S(1)}, f32[160,1536]{1,0:T(8,128)S(1)}, u32[]{:S(2)}, u32[]{:S(2)}) collective-permute-start(f32[160,1536]{1,0:T(8,128)S(1)} %fusion.17), channel_id=1, source_target_pairs={{32,0},{64,32},{96,64},{128,96},{160,128},{192,160},{224,192},{256... | collective-permute-start | bytes 2949128 | tf_op jit(solution)/shard_map/ppermute | solution.py:10
  375.3 105.2 %collective-permute-start.5 = (f32[160,1536]{1,0:T(8,128)S(1)}, f32[160,1536]{1,0:T(8,128)S(1)}, u32[]{:S(2)}, u32[]{:S(2)}) collective-permute-start(f32[160,1536]{1,0:T(8,128)S(1)} %fusion.18), channel_id=1, source_target_pairs={{64,0},{96,32},{128,64},{160,96},{192,128},{224,160},{256,192},{28... | collective-permute-start | bytes 2949128 | tf_op jit(solution)/shard_map/ppermute | solution.py:10
  380.1 100.3 %collective-permute-start.6 = (f32[160,1536]{1,0:T(8,128)S(1)}, f32[160,1536]{1,0:T(8,128)S(1)}, u32[]{:S(2)}, u32[]{:S(2)}) collective-permute-start(f32[160,1536]{1,0:T(8,128)S(1)} %fusion.19), channel_id=1, source_target_pairs={{96,0},{128,32},{160,64},{192,96},{224,128},{256,160},{288,192},{3... | collective-permute-start | bytes 2949128 | tf_op jit(solution)/shard_map/ppermute | solution.py:10
  384.1 96.4 %collective-permute-start.7 = (f32[160,1536]{1,0:T(8,128)S(1)}, f32[160,1536]{1,0:T(8,128)S(1)}, u32[]{:S(2)}, u32[]{:S(2)}) collective-permute-start(f32[160,1536]{1,0:T(8,128)S(1)} %fusion.21), channel_id=1, source_target_pairs={{128,0},{160,32},{192,64},{224,96},{256,128},{288,160},{320,192},{... | collective-permute-start | bytes 2949128 | tf_op jit(solution)/shard_map/ppermute | solution.py:10
  388.3 1.2 copy-start.2
Sparse Core Ops, SparseCore 0:
  116.3 246.7 all-reduce.1
where the time goes:
time: 490 us
  waiting for transfers between devices  415 us (85%)
  starting transfers between devices  38.7 us (8%)
  matrix products  20 us (4%)
  between operations  13.6 us (3%)
    psum x1, waiting for transfers between devices, shards(): summed = lax.psum(jnp.stack(partials), 'grid') / points  247 us
    ppermute x8, waiting for transfers between devices, passed_along(): return lax.ppermute(block, axis, route)  168 us
    ppermute x8, starting transfers between devices, passed_along(): return lax.ppermute(block, axis, route)  38.7 us
    dot_general x14, matrix products, product(): jnp.dot(left, right, precision=lax.Precision.HIGHEST, preferred_element_t...  20 us
  transfers between devices with their start and end apart: 9, of which 5 were waited for; matrix products, arithmetic and copies ran while one was open for 2% of the time, Pallas kernels for 0%

commit v1 on v0

v1 whole, which is shorter than its diff:
```python
import jax
import jax.numpy as jnp
from jax import lax
from jax.sharding import Mesh, PartitionSpec as P

RING = ("xh", "z", "xl")
ROWS, UNIT = 8, 128


def passed_along(block, distance):
    count = lax.axis_size("y")
    return lax.ppermute(block, "y", [(i, (i + distance) % count) for i in range(count)])


def exchange(pieces, axes):
    return lax.all_to_all(pieces, axes, 0, 0)


def spread(piece, axes):
    count = lax.axis_size(axes)
    return exchange(jnp.broadcast_to(piece[None], (count, *piece.shape)), axes)


def product(left, right, dims, precision=lax.Precision.HIGHEST):
    return lax.dot_general(left, right, (dims, ((), ())), precision=precision, preferred_element_type=jnp.float32)


def packed(wide, middle, narrow, single):
    bands = wide.shape[0]
    main = jnp.concatenate(
        [wide, middle[:, :384], narrow[:, :256], single[:, :128], middle[:, 384:], single[:, 128:]], 1
    )
    main = main.reshape(bands // ROWS, ROWS, 12, UNIT).transpose(0, 2, 1, 3).reshape(-1, ROWS, UNIT)
    half = bands // 2
    tail = jnp.concatenate([narrow[:half, 256:], narrow[half:, 256:]], 1).reshape(-1, ROWS, UNIT)
    return jnp.concatenate([main, tail, jnp.zeros((6, ROWS, UNIT), jnp.float32)])


def unpacked(units, bands):
    count = bands // ROWS * 12
    main = units[:count].reshape(bands // ROWS, 12, ROWS, UNIT).transpose(0, 2, 1, 3).reshape(bands, -1)
    tail = units[count : count + 10].reshape(bands // 2, UNIT)
    narrow_end = jnp.concatenate([tail[:, :64], tail[:, 64:]])
    wide = main[:, :640]
    middle = jnp.concatenate([main[:, 640:1024], main[:, 1408:1504]], 1)
    narrow = jnp.concatenate([main[:, 1024:1280], narrow_end], 1)
    single = jnp.concatenate([main[:, 1280:1408], main[:, 1504:]], 1)
    return wide, middle, narrow, single


def scattered(units):
    units = units.reshape(2, -1, ROWS, UNIT)
    units = exchange(units, "c").sum(0)
    units = units.reshape(lax.axis_size(RING), -1, ROWS, UNIT)
    return exchange(units, RING).sum(0)


def shards(orbitals):
    bands = orbitals.shape[0]
    parts = lax.axis_size("xh")
    points = orbitals.shape[1] * lax.axis_size(("z", "xl", "c"))
    row = exchange(orbitals.reshape(bands, parts, -1).transpose(1, 0, 2), "xh")
    below = passed_along(row, 1)
    above = passed_along(row, -1)
    along = ((1,), (1,))
    rows = row.reshape(parts * bands, -1)

    inner = [product(row[a], rows[: bands * (a + 1)], along) for a in range(parts)]
    inner = scattered(packed(inner[3], inner[2], inner[1], inner[0]))

    below, above, inner = lax.optimization_barrier((below, above, inner))
    belows = below.reshape(parts * bands, -1)
    outer = [product(row[a], belows[bands * a :], along) for a in range(parts)]
    outer = scattered(packed(outer[0], outer[1], outer[2], outer[3]))

    share = jnp.stack([inner, outer]) / points
    both = spread(share, RING)
    inner_half = both[:, 0].reshape(-1, ROWS, UNIT)
    outer_half = both[:, 1].reshape(-1, ROWS, UNIT)
    next_half = passed_along(outer_half, -1)
    inner, outer = (
        spread(half, "c").reshape(-1, ROWS, UNIT) for half in (inner_half, outer_half)
    )
    s3, s2, s1, s0 = unpacked(inner, bands)
    inner = [s0, s1, s2, s3]
    outer = unpacked(outer, bands)

    identity = jnp.eye(bands, dtype=jnp.float32)
    stacked = jnp.concatenate([belows, rows, above.reshape(parts * bands, -1)])
    fix = []
    for a in range(parts):
        own = jnp.concatenate([inner[a][:, : bands * a], inner[a][:, bands * a :] - identity], 1)
        left = jnp.concatenate([outer[a], own], 1)
        total = product(left, stacked[bands * a : bands * (a + 5)], ((1,), (0,)))
        if a < parts - 1:
            upper = jnp.concatenate([inner[b][:, bands * a : bands * (a + 1)] for b in range(a + 1, parts)])
            total += product(upper, rows[bands * (a + 1) :], ((0,), (0,)))
        fix.append(total)
    following = unpacked(spread(next_half, "c").reshape(-1, ROWS, UNIT), bands)
    for a in range(parts):
        upper = jnp.concatenate([following[b][:, bands * (a - b) : bands * (a - b + 1)] for b in range(a + 1)])
        fix[a] += product(upper, above.reshape(parts * bands, -1)[: bands * (a + 1)], ((0,), (0,)))
    corrected = row - 0.5 * jnp.stack(fix)
    return exchange(corrected, "xh").transpose(1, 0, 2).reshape(orbitals.shape)


def solution(mesh):
    fine = Mesh(mesh.devices.reshape(8, 4, 8, 2, 2), ("y", "xh", "z", "xl", "c"))
    spec = P(("y", "xh"), ("z", "xl", "c"))
    return jax.shard_map(shards, mesh=fine, in_specs=(spec,), out_specs=spec, check_vma=False)
```

time: 490 us -> 261 us (0.53)
  the two profiles are of different devices: /device:TPU:1 before, /device:TPU:2 now
where the time goes in v1:
time: 261 us; the launch traced here: 260 us
  blocking collectives  85 us (33%)
  waiting for transfers between devices  80.4 us (31%)
  starting transfers between devices  58 us (22%)
  matrix products  18.5 us (7%)
  local copies, waits for them, and re-layouts  13.8 us (5%)
  other arithmetic  3.86 us (1%)
    all_to_all x7, blocking collectives, exchange(): return lax.all_to_all(pieces, axes, 0, 0)  85 us
    all_to_all x3, waiting for transfers between devices, exchange(): return lax.all_to_all(pieces, axes, 0, 0)  62.4 us
    all_to_all x3, starting transfers between devices, exchange(): return lax.all_to_all(pieces, axes, 0, 0)  48.7 us
    dot_general x19, matrix products, product(): lax.dot_general(left, right, (dims, ((), ())), precision=precision, prefe...  18.5 us
    ppermute x3, waiting for transfers between devices, passed_along(): lax.ppermute(block, 'y', [(i, (i + distance) % count) for i in range(coun...  18 us
    ppermute x3, starting transfers between devices, passed_along(): lax.ppermute(block, 'y', [(i, (i + distance) % count) for i in range(coun...  9.35 us
  transfers between devices with their start and end apart: 6, of which 6 were waited for; matrix products, arithmetic and copies ran while one was open for 1% of the time, Pallas kernels for 0%

profile of v1, /device:TPU:2, one launch (start us, length us, event | category | flops | bytes accessed | tf_op | source)
XLA Modules:
  0.0 260.2 jit_solution(2366662869174397311)
XLA Ops:
  0.0 2.2 copy.13
  2.2 5.9 %all-to-all-start = ((f32[4,160,384]{2,1,0:T(8,128)}), f32[4,160,384]{2,1,0:T(8,128)S(1)}, u32[]{:S(2)}, u32[]{:S(2)}) async-start(f32[4,160,384]{2,1,0:T(8,128)} %bitcast.116), calls=%async_computation | async-start | bytes 1966080 | tf_op jit(solution)/shard_map/all_to_all | solution.py:16
  8.1 23.0 %all-to-all-done = f32[4,160,384]{2,1,0:T(8,128)S(1)} async-done(((f32[4,160,384]{2,1,0:T(8,128)}), f32[4,160,384]{2,1,0:T(8,128)S(1)}, u32[]{:S(2)}, u32[]{:S(2)}) %all-to-all-start) | async-done | bytes 983072 | tf_op jit(solution)/shard_map/all_to_all | solution.py:16
  35.3 1.2 fusion.108
  37.0 4.6 %all_to_all.50 = f32[2,128,8,128]{3,2,1,0:T(8,128)S(1)} all-to-all(f32[2,128,8,128]{3,2,1,0:T(8,128)S(1)} %bitcast.150), channel_id=1, replica_groups=mesh['y'=8,'xh'=4,'z'=8,'xl'=2,'c'=2] {'c'}, dimensions={0} | all-to-all | bytes 2097152 | tf_op jit(solution)/shard_map/all_to_all | solution.py:16
  42.5 36.0 %all-to-all-start.2 = ((f32[64,2,8,128]{3,2,1,0:T(8,128)}), f32[64,2,8,128]{3,2,1,0:T(8,128)S(1)}, u32[]{:S(2)}, u32[]{:S(2)}) async-start(f32[64,2,8,128]{3,2,1,0:T(8,128)} %bitcast.13), calls=%async_computation.2 | async-start | bytes 1048576 | tf_op jit(solution)/shard_map/all_to_all | solution.py:16
  78.5 5.4 %collective-permute-start.1 = (f32[4,160,384]{2,1,0:T(8,128)S(1)}, f32[4,160,384]{2,1,0:T(8,128)S(1)}, u32[]{:S(2)}, u32[]{:S(2)}) collective-permute-start(f32[4,160,384]{2,1,0:T(8,128)S(1)} %all-to-all-done), channel_id=1, source_target_pairs={{0,896},{128,0},{256,128},{384,256},{512,384},{640,512},{768,640},... | collective-permute-start | bytes 2949128 | tf_op jit(solution)/shard_map/ppermute | solution.py:12
  83.8 1.9 collective-permute-start
  85.8 10.9 %all-to-all-done.2 = f32[64,2,8,128]{3,2,1,0:T(8,128)S(1)} async-done(((f32[64,2,8,128]{3,2,1,0:T(8,128)}), f32[64,2,8,128]{3,2,1,0:T(8,128)S(1)}, u32[]{:S(2)}, u32[]{:S(2)}) %all-to-all-start.2) | async-done | bytes 524320 | tf_op jit(solution)/shard_map/all_to_all | solution.py:16
  96.7 7.9 %collective-permute-done.1 = f32[4,160,384]{2,1,0:T(8,128)S(1)} collective-permute-done((f32[4,160,384]{2,1,0:T(8,128)S(1)}, f32[4,160,384]{2,1,0:T(8,128)S(1)}, u32[]{:S(2)}, u32[]{:S(2)}) %collective-permute-start.1) | collective-permute-done | bytes 983072 | tf_op jit(solution)/shard_map/ppermute | solution.py:12
  104.6 5.3 %collective-permute-done = f32[4,160,384]{2,1,0:T(8,128)S(1)} collective-permute-done((f32[4,160,384]{2,1,0:T(8,128)S(1)}, f32[4,160,384]{2,1,0:T(8,128)S(1)}, u32[]{:S(2)}, u32[]{:S(2)}) %collective-permute-start) | collective-permute-done | bytes 983072 | tf_op jit(solution)/shard_map/ppermute | solution.py:12
  118.5 4.6 %all_to_all.51 = f32[2,128,8,128]{3,2,1,0:T(8,128)S(1)} all-to-all(f32[2,128,8,128]{3,2,1,0:T(8,128)S(1)} %bitcast.149), channel_id=1, replica_groups=mesh['y'=8,'xh'=4,'z'=8,'xl'=2,'c'=2] {'c'}, dimensions={0} | all-to-all | bytes 2097152 | tf_op jit(solution)/shard_map/all_to_all | solution.py:16
  123.2 30.7 %all_to_all.52 = f32[64,2,8,128]{3,2,1,0:T(8,128)S(1)} all-to-all(f32[64,2,8,128]{3,2,1,0:T(8,128)S(1)} %bitcast.169), channel_id=1, replica_groups=mesh['y'=8,'xh'=4,'z'=8,'xl'=2,'c'=2] {'xh','z','xl'}, dimensions={0} | all-to-all | bytes 1048576 | tf_op jit(solution)/shard_map/all_to_all | solution.py:16
  155.1 6.8 %all-to-all-start.5 = ((f32[64,2,2,8,128]{4,3,2,1,0:T(8,128)}), f32[64,2,2,8,128]{4,3,2,1,0:T(8,128)S(1)}, u32[]{:S(2)}, u32[]{:S(2)}) async-start(f32[64,2,2,8,128]{4,3,2,1,0:T(8,128)} %broadcast_in_dim.12), calls=%async_computation.5 | async-start | bytes 2097152 | tf_op jit(solution)/shard_map/all_to_all | solution.py:16
  161.9 28.6 %all-to-all-done.5 = f32[64,2,2,8,128]{4,3,2,1,0:T(8,128)S(1)} async-done(((f32[64,2,2,8,128]{4,3,2,1,0:T(8,128)}), f32[64,2,2,8,128]{4,3,2,1,0:T(8,128)S(1)}, u32[]{:S(2)}, u32[]{:S(2)}) %all-to-all-start.5) | async-done | bytes 1048608 | tf_op jit(solution)/shard_map/all_to_all | solution.py:16
  190.7 4.6 %all_to_all.53 = f32[2,128,8,128]{3,2,1,0:T(8,128)S(1)} all-to-all(f32[2,128,8,128]{3,2,1,0:T(8,128)S(1)} %broadcast_in_dim.30), channel_id=1, replica_groups=mesh['y'=8,'xh'=4,'z'=8,'xl'=2,'c'=2] {'c'}, dimensions={0} | all-to-all | bytes 2097152 | tf_op jit(solution)/shard_map/all_to_all | solution.py:16
  195.6 2.1 collective-permute-start.2
  197.7 4.6 %all_to_all.54 = f32[2,128,8,128]{3,2,1,0:T(8,128)S(1)} all-to-all(f32[2,128,8,128]{3,2,1,0:T(8,128)S(1)} %broadcast_in_dim.28), channel_id=1, replica_groups=mesh['y'=8,'xh'=4,'z'=8,'xl'=2,'c'=2] {'c'}, dimensions={0} | all-to-all | bytes 2097152 | tf_op jit(solution)/shard_map/all_to_all | solution.py:16
  206.7 4.8 %collective-permute-done.2 = f32[128,8,128]{2,1,0:T(8,128)S(1)} collective-permute-done((f32[128,8,128]{2,1,0:T(8,128)S(1)}, f32[128,8,128]{2,1,0:T(8,128)S(1)}, u32[]{:S(2)}, u32[]{:S(2)}) %collective-permute-start.2) | collective-permute-done | bytes 524320 | tf_op jit(solution)/shard_map/ppermute | solution.py:12
  211.6 4.6 %all_to_all.55 = f32[2,128,8,128]{3,2,1,0:T(8,128)S(1)} all-to-all(f32[2,128,8,128]{3,2,1,0:T(8,128)S(1)} %broadcast_in_dim.31), channel_id=1, replica_groups=mesh['y'=8,'xh'=4,'z'=8,'xl'=2,'c'=2] {'c'}, dimensions={0} | all-to-all | bytes 2097152 | tf_op jit(solution)/shard_map/all_to_all | solution.py:16
  222.3 1.5 fusion.43
  223.9 1.3 fusion.12
  226.4 1.2 fusion.37
  227.7 31.4 %all_to_all.56 = f32[4,160,384]{2,1,0:T(8,128)S(1)} all-to-all(f32[4,160,384]{2,1,0:T(8,128)S(1)} %fusion.40), channel_id=1, replica_groups=mesh['y'=8,'xh'=4,'z'=8,'xl'=2,'c'=2] {'xh'}, dimensions={0} | all-to-all | bytes 1966080 | tf_op jit(solution)/shard_map/all_to_all | solution.py:16
  (107 shorter events, 28.7 us)
Async XLA Ops:
  2.2 28.9 %all-to-all-start = ((f32[4,160,384]{2,1,0:T(8,128)}), f32[4,160,384]{2,1,0:T(8,128)S(1)}, u32[]{:S(2)}, u32[]{:S(2)}) async-start(f32[4,160,384]{2,1,0:T(8,128)} %bitcast.116), calls=%async_computation | async-start | bytes 1966080 | tf_op jit(solution)/shard_map/all_to_all | solution.py:16
  31.5 0.9 copy-start.6
  33.2 1.0 copy-start.5
  35.1 1.4 slice-start.2
  35.1 1.4 slice-start.3
  35.2 1.4 slice-start.4
  42.5 54.2 %all-to-all-start.2 = ((f32[64,2,8,128]{3,2,1,0:T(8,128)}), f32[64,2,8,128]{3,2,1,0:T(8,128)S(1)}, u32[]{:S(2)}, u32[]{:S(2)}) async-start(f32[64,2,8,128]{3,2,1,0:T(8,128)} %bitcast.13), calls=%async_computation.2 | async-start | bytes 1048576 | tf_op jit(solution)/shard_map/all_to_all | solution.py:16
  78.5 26.1 %collective-permute-start.1 = (f32[4,160,384]{2,1,0:T(8,128)S(1)}, f32[4,160,384]{2,1,0:T(8,128)S(1)}, u32[]{:S(2)}, u32[]{:S(2)}) collective-permute-start(f32[4,160,384]{2,1,0:T(8,128)S(1)} %all-to-all-done), channel_id=1, source_target_pairs={{0,896},{128,0},{256,128},{384,256},{512,384},{640,512},{768,640},... | collective-permute-start | bytes 2949128 | tf_op jit(solution)/shard_map/ppermute | solution.py:12
  83.8 26.1 %collective-permute-start = (f32[4,160,384]{2,1,0:T(8,128)S(1)}, f32[4,160,384]{2,1,0:T(8,128)S(1)}, u32[]{:S(2)}, u32[]{:S(2)}) collective-permute-start(f32[4,160,384]{2,1,0:T(8,128)S(1)} %all-to-all-done), channel_id=1, source_target_pairs={{0,128},{128,256},{256,384},{384,512},{512,640},{640,768},{768,896... | collective-permute-start | bytes 2949128 | tf_op jit(solution)/shard_map/ppermute | solution.py:12
  104.6 6.6 %copy-start.1 = (f32[4,160,384]{2,1,0:T(8,128)}, f32[4,160,384]{2,1,0:T(8,128)S(1)}, u32[]{:S(2)}) copy-start(f32[4,160,384]{2,1,0:T(8,128)S(1)} %collective-permute-done.1) | copy-start | bytes 2949124
  110.3 0.8 copy-start.7
  113.5 2.6 %slice-start.5 = ((f32[160,160]{1,0:T(8,128)}), f32[160,32]{1,0:T(8,128)S(1)}, s32[]{:S(2)}) async-start(f32[160,160]{1,0:T(8,128)} %copy-done.7), calls=%async_computation.15 | async-start | bytes 163840 | tf_op jit(solution)/shard_map/slice | solution.py:31
  113.5 2.7 %slice-start.6 = ((f32[160,160]{1,0:T(8,128)}), f32[160,128]{1,0:T(8,128)S(1)}, s32[]{:S(2)}) async-start(f32[160,160]{1,0:T(8,128)} %copy-done.7), calls=%async_computation.16 | async-start | bytes 163840 | tf_op jit(solution)/shard_map/slice | solution.py:31
  155.1 35.4 %all-to-all-start.5 = ((f32[64,2,2,8,128]{4,3,2,1,0:T(8,128)}), f32[64,2,2,8,128]{4,3,2,1,0:T(8,128)S(1)}, u32[]{:S(2)}, u32[]{:S(2)}) async-start(f32[64,2,2,8,128]{4,3,2,1,0:T(8,128)} %broadcast_in_dim.12), calls=%async_computation.5 | async-start | bytes 2097152 | tf_op jit(solution)/shard_map/all_to_all | solution.py:16
  195.6 15.9 %collective-permute-start.2 = (f32[128,8,128]{2,1,0:T(8,128)S(1)}, f32[128,8,128]{2,1,0:T(8,128)S(1)}, u32[]{:S(2)}, u32[]{:S(2)}) collective-permute-start(f32[128,8,128]{2,1,0:T(8,128)S(1)} %bitcast.166), channel_id=1, source_target_pairs={{0,896},{128,0},{256,128},{384,256},{512,384},{640,512},{768,640},... | collective-permute-start | bytes 1572872 | tf_op jit(solution)/shard_map/ppermute | solution.py:12
  203.6 1.0 copy-start.4
  203.8 1.7 copy-start
  216.2 1.2 copy-start.2
  218.0 1.0 slice-start
  218.3 1.6 slice-start.1
  221.0 1.3 copy-start.3

commit v2 on v0

v2 whole, which is shorter than its diff:
```python
import functools

import jax
import jax.numpy as jnp
from jax import lax
from jax.experimental import pallas as pl
from jax.experimental.pallas import tpu as pltpu
from jax.sharding import Mesh, PartitionSpec as P

RING = ("xh", "z", "xl")
ROWS, UNIT = 8, 128
GROUPS = 4
UNITS = 256
NT = ((1,), (1,))
NN = ((1,), (0,))
TN = ((0,), (0,))


def passed_along(block, distance):
    count = lax.axis_size("y")
    return lax.ppermute(block, "y", [(i, (i + distance) % count) for i in range(count)])


def exchange(pieces, axes):
    return lax.all_to_all(pieces, axes, 0, 0)


def spread(piece, axes):
    count = lax.axis_size(axes)
    return exchange(jnp.broadcast_to(piece[None], (count, *piece.shape)), axes)


def halves(value):
    high = value.astype(jnp.bfloat16)
    return high, (value - high.astype(jnp.float32)).astype(jnp.bfloat16)


def product(left, right, dims):
    dot = functools.partial(
        lax.dot_general, dimension_numbers=(dims, ((), ())), preferred_element_type=jnp.float32
    )
    return dot(left[0], right[0]) + (dot(left[0], right[1]) + dot(left[1], right[0]))


def cut(pair, rows=slice(None), columns=slice(None)):
    return tuple(value[rows, columns] for value in pair)


def call(kernel, outs, *operands):
    return pl.pallas_call(
        kernel,
        out_shape=jax.ShapeDtypeStruct(outs, jnp.float32),
        compiler_params=pltpu.CompilerParams(vmem_limit_bytes=48 << 20),
    )(*operands)


def tiles_kernel(order, row_ref, other_ref, units_ref):
    bands = row_ref.shape[1]
    other = halves(other_ref[...].reshape(GROUPS * bands, -1))

    def put(index, value):
        count = value.shape[0] // ROWS
        units_ref[20 * index : 20 * index + count] = value.reshape(count, ROWS, UNIT)

    strips = []
    for a, first, last in order:
        left = halves(row_ref[a])
        strips.append(product(left, cut(other, slice(bands * first, bands * last)), NT))
    wide, middle, narrow, single = strips
    columns = [wide[:, UNIT * i : UNIT * (i + 1)] for i in range(5)]
    columns += [middle[:, UNIT * i : UNIT * (i + 1)] for i in range(3)]
    columns += [narrow[:, UNIT * i : UNIT * (i + 1)] for i in range(2)]
    columns += [single[:, :UNIT], jnp.concatenate([middle[:, 384:], single[:, UNIT:]], 1)]
    columns += [jnp.concatenate([narrow[: bands // 2, 256:], narrow[bands // 2 :, 256:]], 1)]
    for index, value in enumerate(columns):
        put(index, value)
    units_ref[250:] = jnp.zeros((6, ROWS, UNIT), jnp.float32)


def strips_of(units_ref, offset):
    half = UNITS // 2

    def get(index, count=20):
        start, stop = 20 * index, 20 * index + count
        parts = []
        for core in range(2):
            low, high = max(start, half * core) - half * core, min(stop, half * (core + 1)) - half * core
            if low < high:
                part = units_ref[core, low // 2 : high // 2, offset : offset + 2]
                parts.append(part.reshape(high - low, ROWS, UNIT))
        value = parts[0] if len(parts) == 1 else jnp.concatenate(parts)
        return value.reshape(count * ROWS, UNIT)

    mixed, tail = get(11), get(12, 10)
    wide = jnp.concatenate([get(i) for i in range(5)], 1)
    middle = jnp.concatenate([get(5), get(6), get(7), mixed[:, :96]], 1)
    narrow = jnp.concatenate([get(8), get(9), jnp.concatenate([tail[:, :64], tail[:, 64:]])], 1)
    single = jnp.concatenate([get(10), mixed[:, 96:]], 1)
    return wide, middle, narrow, single


def apply_kernel(row_ref, below_ref, units_ref, out_ref):
    bands = row_ref.shape[1]
    rows = halves(row_ref[...].reshape(GROUPS * bands, -1))
    below = halves(below_ref[...].reshape(GROUPS * bands, -1))
    inner = strips_of(units_ref, 0)[::-1]
    outer = strips_of(units_ref, 2)
    fix = []
    for a in range(GROUPS):
        width = bands * (a + 1)
        shift = lax.broadcasted_iota(jnp.int32, (bands, width), 1) - lax.broadcasted_iota(
            jnp.int32, (bands, width), 0
        )
        own = halves(jnp.where(shift == bands * a, inner[a] - 1.0, inner[a]))
        total = product(own, cut(rows, slice(0, width)), NN)
        total += product(halves(outer[a]), cut(below, slice(bands * a, None)), NN)
        fix.append(total)
        if a > 0:
            back = product(
                cut(own, slice(None), slice(0, bands * a)), cut(rows, slice(bands * a, width)), TN
            )
            for b in range(a):
                fix[b] += back[bands * b : bands * (b + 1)]
    for a in range(GROUPS):
        out_ref[a] = row_ref[a] - 0.5 * fix[a]


def above_kernel(part_ref, above_ref, units_ref, out_ref):
    bands = part_ref.shape[1]
    above = halves(above_ref[...].reshape(GROUPS * bands, -1))
    strips = strips_of(units_ref, 0)
    fix = [None] * GROUPS
    for b in range(GROUPS):
        back = product(halves(strips[b]), cut(above, slice(bands * b, bands * (b + 1))), TN)
        for a in range(b, GROUPS):
            term = back[bands * (a - b) : bands * (a - b + 1)]
            fix[a] = term if b == 0 else fix[a] + term
    for a in range(GROUPS):
        out_ref[a] = part_ref[a] - 0.5 * fix[a]


INNER = [(3, 0, 4), (2, 0, 3), (1, 0, 2), (0, 0, 1)]
OUTER = [(0, 0, 4), (1, 1, 4), (2, 2, 4), (3, 3, 4)]


def shards(orbitals):
    bands = orbitals.shape[0]
    points = orbitals.shape[1] * lax.axis_size(("z", "xl", "c"))
    members = lax.axis_size(RING)
    row = exchange(orbitals.reshape(bands, GROUPS, -1).transpose(1, 0, 2), "xh")
    below = passed_along(row, 1)
    above = passed_along(row, -1)

    def tiles(order, other):
        units = call(functools.partial(tiles_kernel, order), (UNITS, ROWS, UNIT), row, other)
        pair = exchange(units.reshape(2, UNITS // 2, ROWS, UNIT), "c")
        return (pair[0] + pair[1]).reshape(members, -1, ROWS, UNIT)

    inner = tiles(INNER, row)
    below, above, inner = lax.optimization_barrier((below, above, inner))
    outer = tiles(OUTER, below)
    share = exchange(jnp.concatenate([inner, outer], 1), RING).sum(0) / points

    both = spread(share, RING)
    following = passed_along(both[:, 2:], -1)
    part = call(apply_kernel, row.shape, row, below, spread(both, "c"))
    corrected = call(above_kernel, row.shape, part, above, spread(following, "c"))
    return exchange(corrected, "xh").transpose(1, 0, 2).reshape(orbitals.shape)


def solution(mesh):
    fine = Mesh(mesh.devices.reshape(8, 4, 8, 2, 2), ("y", "xh", "z", "xl", "c"))
    spec = P(("y", "xh"), ("z", "xl", "c"))
    return jax.shard_map(shards, mesh=fine, in_specs=(spec,), out_specs=spec, check_vma=False)
```

time: 490 us -> 222 us (0.45)
  the two profiles are of different devices: /device:TPU:1 before, /device:TPU:2 now
where the time goes in v2:
time: 222 us
  blocking collectives  180 us (81%)
  waiting for transfers between devices  15 us (7%)
  starting transfers between devices  14.8 us (7%)
  Pallas kernels  7.44 us (3%)
  local copies, waits for them, and re-layouts  2.83 us (1%)
    all_to_all x8, blocking collectives, exchange(): return lax.all_to_all(pieces, axes, 0, 0)  180 us
    ppermute x3, waiting for transfers between devices, passed_along(): lax.ppermute(block, 'y', [(i, (i + distance) % count) for i in range(coun...  15 us
    ppermute x3, starting transfers between devices, passed_along(): lax.ppermute(block, 'y', [(i, (i + distance) % count) for i in range(coun...  14.8 us
    pallas_call x4, Pallas kernels, call(): pl.pallas_call(kernel, out_shape=jax.ShapeDtypeStruct(outs, jnp.float32),...  7.44 us
  transfers between devices with their start and end apart: 3, of which 3 were waited for; matrix products, arithmetic and copies ran while one was open for 0% of the time, Pallas kernels for 2%

profile of v2, /device:TPU:2, one launch (start us, length us, event | category | flops | bytes accessed | tf_op | source)
XLA Modules:
  0.0 221.9 jit_solution(12397542106292166220)
XLA Ops:
  0.0 1.3 copy.7
  1.3 28.0 %all_to_all.40.row_ref.other_ref = f32[4,160,384]{2,1,0:T(8,128)S(1)} all-to-all(f32[4,160,384]{2,1,0:T(8,128)S(1)} %bitcast.17), channel_id=1, replica_groups=mesh['y'=8,'xh'=4,'z'=8,'xl'=2,'c'=2] {'xh'}, dimensions={0} | all-to-all | bytes 1966080 | tf_op jit(solution)/shard_map/all_to_all | solution.py:25
  29.3 10.9 %collective-permute-start.1 = (f32[4,160,384]{2,1,0:T(8,128)S(1)}, f32[4,160,384]{2,1,0:T(8,128)S(1)}, u32[]{:S(2)}, u32[]{:S(2)}) collective-permute-start(f32[4,160,384]{2,1,0:T(8,128)S(1)} %all_to_all.40.row_ref.other_ref), channel_id=1, source_target_pairs={{0,896},{128,0},{256,128},{384,256},{512,384},{640,512},{768,640},... | collective-permute-start | bytes 2949128 | tf_op jit(solution)/shard_map/ppermute | solution.py:21
  40.2 1.9 collective-permute-start
  42.1 1.5 shard_map.17
  43.7 4.6 %all_to_all.41 = f32[2,128,8,128]{3,2,1,0:T(8,128)S(1)} all-to-all(f32[2,128,8,128]{3,2,1,0:T(8,128)S(1)} %bitcast.14), channel_id=1, replica_groups=mesh['y'=8,'xh'=4,'z'=8,'xl'=2,'c'=2] {'c'}, dimensions={0} | all-to-all | bytes 2097152 | tf_op jit(solution)/shard_map/all_to_all | solution.py:25
  48.3 6.6 %collective-permute-done.1.above_ref = f32[4,160,384]{2,1,0:T(8,128)S(1)} collective-permute-done((f32[4,160,384]{2,1,0:T(8,128)S(1)}, f32[4,160,384]{2,1,0:T(8,128)S(1)}, u32[]{:S(2)}, u32[]{:S(2)}) %collective-permute-start.1) | collective-permute-done | bytes 983072 | tf_op jit(solution)/shard_map/ppermute | solution.py:21
  54.9 5.3 %collective-permute-done.other_ref.below_ref = f32[4,160,384]{2,1,0:T(8,128)S(1)} collective-permute-done((f32[4,160,384]{2,1,0:T(8,128)S(1)}, f32[4,160,384]{2,1,0:T(8,128)S(1)}, u32[]{:S(2)}, u32[]{:S(2)}) %collective-permute-start) | collective-permute-done | bytes 983072 | tf_op jit(solution)/shard_map/ppermute | solution.py:21
  60.2 1.5 shard_map.18
  61.8 4.6 %all_to_all.42 = f32[2,128,8,128]{3,2,1,0:T(8,128)S(1)} all-to-all(f32[2,128,8,128]{3,2,1,0:T(8,128)S(1)} %bitcast.15), channel_id=1, replica_groups=mesh['y'=8,'xh'=4,'z'=8,'xl'=2,'c'=2] {'c'}, dimensions={0} | all-to-all | bytes 2097152 | tf_op jit(solution)/shard_map/all_to_all | solution.py:25
  66.4 0.1 pad_maximum_fusion
  66.5 65.7 %all_to_all.43 = f32[64,4,8,128]{3,2,1,0:T(8,128)} all-to-all(f32[64,4,8,128]{3,2,1,0:T(8,128)S(1)} %pad_maximum_fusion), channel_id=1, replica_groups=mesh['y'=8,'xh'=4,'z'=8,'xl'=2,'c'=2] {'xh','z','xl'}, dimensions={0} | all-to-all | bytes 2097152 | tf_op jit(solution)/shard_map/all_to_all | solution.py:25
  132.3 1.3 reduce_sum.9
  133.6 0.1 broadcast_in_dim.6
  133.7 35.7 %all_to_all.44 = f32[64,4,8,128]{3,2,1,0:T(8,128)S(1)} all-to-all(f32[64,4,8,128]{3,2,1,0:T(8,128)S(1)} %broadcast_in_dim.6), channel_id=1, replica_groups=mesh['y'=8,'xh'=4,'z'=8,'xl'=2,'c'=2] {'xh','z','xl'}, dimensions={0} | all-to-all | bytes 2097152 | tf_op jit(solution)/shard_map/all_to_all | solution.py:25
  169.5 1.9 collective-permute-start.2
  171.4 0.3 broadcast_in_dim.7
  171.7 5.4 %all_to_all.45.units_ref = f32[2,64,4,8,128]{4,3,2,1,0:T(8,128)S(1)} all-to-all(f32[2,64,4,8,128]{4,3,2,1,0:T(8,128)S(1)} %broadcast_in_dim.7), channel_id=1, replica_groups=mesh['y'=8,'xh'=4,'z'=8,'xl'=2,'c'=2] {'c'}, dimensions={0} | all-to-all | bytes 4194304 | tf_op jit(solution)/shard_map/all_to_all | solution.py:25
  177.1 2.9 %shard_map.19.part_ref = f32[4,160,384]{2,1,0:T(8,128)S(1)} custom-call(f32[4,160,384]{2,1,0:T(8,128)S(1)} %all_to_all.40.row_ref.other_ref, f32[4,160,384]{2,1,0:T(8,128)S(1)} %collective-permute-done.other_ref.below_ref, f32[2,64,4,8,128]{4,3,2,1,0:T(8,128)S(1)} %all_to_all.45.units_ref), custom_call_target="tpu_custom_call" | custom-call | tf_op jit(solution)/shard_map/pallas_call | solution.py:50
  180.1 3.1 %collective-permute-done.2 = f32[64,2,8,128]{3,2,1,0:T(8,128)S(1)} collective-permute-done((f32[64,2,8,128]{3,2,1,0:T(8,128)S(1)}, f32[64,2,8,128]{3,2,1,0:T(8,128)S(1)}, u32[]{:S(2)}, u32[]{:S(2)}) %collective-permute-start.2) | collective-permute-done | bytes 524320 | tf_op jit(solution)/shard_map/ppermute | solution.py:21
  183.2 4.6 %all_to_all.46.units_ref = f32[2,64,2,8,128]{4,3,2,1,0:T(8,128)S(1)} all-to-all(f32[2,64,2,8,128]{4,3,2,1,0:T(8,128)S(1)} %broadcast_in_dim.8), channel_id=1, replica_groups=mesh['y'=8,'xh'=4,'z'=8,'xl'=2,'c'=2] {'c'}, dimensions={0} | all-to-all | bytes 2097152 | tf_op jit(solution)/shard_map/all_to_all | solution.py:25
  187.8 1.5 shard_map.20
  189.3 31.5 %all_to_all.47 = f32[4,160,384]{2,1,0:T(8,128)S(1)} all-to-all(f32[4,160,384]{2,1,0:T(8,128)S(1)} %shard_map.20), channel_id=1, replica_groups=mesh['y'=8,'xh'=4,'z'=8,'xl'=2,'c'=2] {'xh'}, dimensions={0} | all-to-all | bytes 1966080 | tf_op jit(solution)/shard_map/all_to_all | solution.py:25
  220.8 1.1 copy.5
  (5 shorter events, 0.2 us)
Async XLA Ops:
  29.3 25.6 %collective-permute-start.1 = (f32[4,160,384]{2,1,0:T(8,128)S(1)}, f32[4,160,384]{2,1,0:T(8,128)S(1)}, u32[]{:S(2)}, u32[]{:S(2)}) collective-permute-start(f32[4,160,384]{2,1,0:T(8,128)S(1)} %all_to_all.40.row_ref.other_ref), channel_id=1, source_target_pairs={{0,896},{128,0},{256,128},{384,256},{512,384},{640,512},{768,640},... | collective-permute-start | bytes 2949128 | tf_op jit(solution)/shard_map/ppermute | solution.py:21
  40.2 20.0 %collective-permute-start = (f32[4,160,384]{2,1,0:T(8,128)S(1)}, f32[4,160,384]{2,1,0:T(8,128)S(1)}, u32[]{:S(2)}, u32[]{:S(2)}) collective-permute-start(f32[4,160,384]{2,1,0:T(8,128)S(1)} %all_to_all.40.row_ref.other_ref), channel_id=1, source_target_pairs={{0,128},{128,256},{256,384},{384,512},{512,640},{640,768},{768,896... | collective-permute-start | bytes 2949128 | tf_op jit(solution)/shard_map/ppermute | solution.py:21
  169.5 13.7 %collective-permute-start.2 = (f32[64,2,8,128]{3,2,1,0:T(8,128)S(1)}, f32[64,2,8,128]{3,2,1,0:T(8,128)S(1)}, u32[]{:S(2)}, u32[]{:S(2)}) collective-permute-start(f32[64,2,8,128]{3,2,1,0:T(8,128)S(1)} %slice.24), channel_id=1, source_target_pairs={{0,896},{128,0},{256,128},{384,256},{512,384},{640,512},{768,640},... | collective-permute-start | bytes 1572872 | tf_op jit(solution)/shard_map/ppermute | solution.py:21

commit v3 on v2

--- a/solution.py
+++ b/solution.py
@@ -6,6 +6,7 @@
 from jax.experimental import pallas as pl
 from jax.experimental.pallas import tpu as pltpu
 from jax.sharding import Mesh, PartitionSpec as P
+
 
 RING = ("xh", "z", "xl")
 ROWS, UNIT = 8, 128
@@ -54,9 +55,16 @@
     )(*operands)
 
 
-def tiles_kernel(order, row_ref, other_ref, units_ref):
-    bands = row_ref.shape[1]
-    other = halves(other_ref[...].reshape(GROUPS * bands, -1))
+def joined(head_ref, tail_ref):
+    value = jnp.concatenate([head_ref[...], tail_ref[...]], -1)
+    return value.reshape(-1, value.shape[-1])
+
+
+def tiles_kernel(order, row_head, row_tail, *refs):
+    *other_refs, units_ref = refs
+    bands = row_head.shape[1]
+    rows = halves(joined(row_head, row_tail))
+    other = halves(joined(*other_refs)) if other_refs else rows
 
     def put(index, value):
         count = value.shape[0] // ROWS
@@ -64,7 +72,7 @@
 
     strips = []
     for a, first, last in order:
-        left = halves(row_ref[a])
+        left = cut(rows, slice(bands * a, bands * (a + 1)))
         strips.append(product(left, cut(other, slice(bands * first, bands * last)), NT))
     wide, middle, narrow, single = strips
     columns = [wide[:, UNIT * i : UNIT * (i + 1)] for i in range(5)]
@@ -99,10 +107,11 @@
     return wide, middle, narrow, single
 
 
-def apply_kernel(row_ref, below_ref, units_ref, out_ref):
-    bands = row_ref.shape[1]
-    rows = halves(row_ref[...].reshape(GROUPS * bands, -1))
-    below = halves(below_ref[...].reshape(GROUPS * bands, -1))
+def apply_kernel(row_head, row_tail, below_head, below_tail, units_ref, out_ref):
+    bands = row_head.shape[1]
+    row = joined(row_head, row_tail)
+    rows = halves(row)
+    below = halves(joined(below_head, below_tail))
     inner = strips_of(units_ref, 0)[::-1]
     outer = strips_of(units_ref, 2)
     fix = []
@@ -122,12 +131,12 @@
             for b in range(a):
                 fix[b] += back[bands * b : bands * (b + 1)]
     for a in range(GROUPS):
-        out_ref[a] = row_ref[a] - 0.5 * fix[a]
+        out_ref[a] = row[bands * a : bands * (a + 1)] - 0.5 * fix[a]
 
 
-def above_kernel(part_ref, above_ref, units_ref, out_ref):
+def above_kernel(part_ref, above_head, above_tail, units_ref, out_ref):
     bands = part_ref.shape[1]
-    above = halves(above_ref[...].reshape(GROUPS * bands, -1))
+    above = halves(joined(above_head, above_tail))
     strips = strips_of(units_ref, 0)
     fix = [None] * GROUPS
     for b in range(GROUPS):
@@ -147,24 +156,31 @@
     bands = orbitals.shape[0]
     points = orbitals.shape[1] * lax.axis_size(("z", "xl", "c"))
     members = lax.axis_size(RING)
-    row = exchange(orbitals.reshape(bands, GROUPS, -1).transpose(1, 0, 2), "xh")
-    below = passed_along(row, 1)
-    above = passed_along(row, -1)
+    width = orbitals.shape[1] // GROUPS
+    split = width // 3 * 2
+    pieces = [orbitals[:, width * a : width * (a + 1)] for a in range(GROUPS)]
+    head = exchange(jnp.stack([piece[:, :split] for piece in pieces]), "xh")
+    below_head = passed_along(head, 1)
+    tail = exchange(jnp.stack([piece[:, split:] for piece in pieces]), "xh")
+    below_tail = passed_along(tail, 1)
+    above_head = passed_along(head, -1)
+    above_tail = passed_along(tail, -1)
 
-    def tiles(order, other):
-        units = call(functools.partial(tiles_kernel, order), (UNITS, ROWS, UNIT), row, other)
+    def tiles(order, *operands):
+        units = call(functools.partial(tiles_kernel, order), (UNITS, ROWS, UNIT), *operands)
         pair = exchange(units.reshape(2, UNITS // 2, ROWS, UNIT), "c")
         return (pair[0] + pair[1]).reshape(members, -1, ROWS, UNIT)
 
-    inner = tiles(INNER, row)
-    below, above, inner = lax.optimization_barrier((below, above, inner))
-    outer = tiles(OUTER, below)
-    share = exchange(jnp.concatenate([inner, outer], 1), RING).sum(0) / points
-
+    inner = tiles(INNER, head, tail)
+    below_head, below_tail, inner = lax.optimization_barrier((below_head, below_tail, inner))
+    outer = tiles(OUTER, head, tail, below_head, below_tail)
+    share = exchange(jnp.concatenate([inner, outer], 1), RING)
+    share = share.sum(0) / points
     both = spread(share, RING)
     following = passed_along(both[:, 2:], -1)
-    part = call(apply_kernel, row.shape, row, below, spread(both, "c"))
-    corrected = call(above_kernel, row.shape, part, above, spread(following, "c"))
+    shape = (GROUPS, bands, width)
+    part = call(apply_kernel, shape, head, tail, below_head, below_tail, spread(both, "c"))
+    corrected = call(above_kernel, shape, part, above_head, above_tail, spread(following, "c"))
     return exchange(corrected, "xh").transpose(1, 0, 2).reshape(orbitals.shape)
 
 

time: 222 us -> 221 us (level)
  the two profiles are of different devices: /device:TPU:2 before, /device:TPU:48 now
where the time goes in v3:
time: 221 us
  blocking collectives  107 us (48%)
  waiting for transfers between devices  59.6 us (27%)
  starting transfers between devices  38 us (17%)
  Pallas kernels  8.52 us (4%)
  local copies, waits for them, and re-layouts  5.72 us (3%)
    all_to_all x5, blocking collectives, exchange(): return lax.all_to_all(pieces, axes, 0, 0)  107 us
    all_to_all x4, waiting for transfers between devices, exchange(): return lax.all_to_all(pieces, axes, 0, 0)  51 us
    all_to_all x4, starting transfers between devices, exchange(): return lax.all_to_all(pieces, axes, 0, 0)  22 us
    ppermute x5, starting transfers between devices, passed_along(): lax.ppermute(block, 'y', [(i, (i + distance) % count) for i in range(coun...  16 us
    ppermute x5, waiting for transfers between devices, passed_along(): lax.ppermute(block, 'y', [(i, (i + distance) % count) for i in range(coun...  8.55 us
    pallas_call x4, Pallas kernels, call(): pl.pallas_call(kernel, out_shape=jax.ShapeDtypeStruct(outs, jnp.float32),...  8.52 us
  transfers between devices with their start and end apart: 9, of which 6 were waited for; matrix products, arithmetic and copies ran while one was open for 1% of the time, Pallas kernels for 2%

profile of v3, /device:TPU:48, one launch (start us, length us, event | category | flops | bytes accessed | tf_op | source)
XLA Modules:
  0.0 220.7 jit_solution(7118932311249138120)
XLA Ops:
  2.1 6.8 %all-to-all-start = ((f32[4,160,256]{2,1,0:T(8,128)}), f32[4,160,256]{2,1,0:T(8,128)S(1)}, u32[]{:S(2)}, u32[]{:S(2)}) async-start(f32[4,160,256]{2,1,0:T(8,128)} %pad_maximum_fusion.1), calls=%async_computation | async-start | bytes 1310720 | tf_op jit(solution)/shard_map/all_to_all | solution.py:26
  10.6 16.3 %all-to-all-done.row_head = f32[4,160,256]{2,1,0:T(8,128)S(1)} async-done(((f32[4,160,256]{2,1,0:T(8,128)}), f32[4,160,256]{2,1,0:T(8,128)S(1)}, u32[]{:S(2)}, u32[]{:S(2)}) %all-to-all-start) | async-done | bytes 655392 | tf_op jit(solution)/shard_map/all_to_all | solution.py:26
  26.9 4.1 %all-to-all-start.1 = ((f32[4,160,128]{2,1,0:T(8,128)}), f32[4,160,128]{2,1,0:T(8,128)S(1)}, u32[]{:S(2)}, u32[]{:S(2)}) async-start(f32[4,160,128]{2,1,0:T(8,128)} %pad_maximum_fusion.2), calls=%async_computation.1 | async-start | bytes 655360 | tf_op jit(solution)/shard_map/all_to_all | solution.py:26
  31.0 4.8 %collective-permute-start = (f32[4,160,256]{2,1,0:T(8,128)S(1)}, f32[4,160,256]{2,1,0:T(8,128)S(1)}, u32[]{:S(2)}, u32[]{:S(2)}) collective-permute-start(f32[4,160,256]{2,1,0:T(8,128)S(1)} %all-to-all-done.row_head), channel_id=1, source_target_pairs={{0,128},{128,256},{256,384},{384,512},{512,640},{640,768},{768,896... | collective-permute-start | bytes 1966088 | tf_op jit(solution)/shard_map/ppermute | solution.py:22
  35.8 6.5 %all-to-all-done.1.row_tail = f32[4,160,128]{2,1,0:T(8,128)S(1)} async-done(((f32[4,160,128]{2,1,0:T(8,128)}), f32[4,160,128]{2,1,0:T(8,128)S(1)}, u32[]{:S(2)}, u32[]{:S(2)}) %all-to-all-start.1) | async-done | bytes 327712 | tf_op jit(solution)/shard_map/all_to_all | solution.py:26
  42.3 4.8 %collective-permute-start.1 = (f32[4,160,128]{2,1,0:T(8,128)S(1)}, f32[4,160,128]{2,1,0:T(8,128)S(1)}, u32[]{:S(2)}, u32[]{:S(2)}) collective-permute-start(f32[4,160,128]{2,1,0:T(8,128)S(1)} %all-to-all-done.1.row_tail), channel_id=1, source_target_pairs={{0,128},{128,256},{256,384},{384,512},{512,640},{640,768},{768,896... | collective-permute-start | bytes 983048 | tf_op jit(solution)/shard_map/ppermute | solution.py:22
  47.1 1.5 shard_map.17
  48.6 4.6 %all_to_all.45 = f32[2,128,8,128]{3,2,1,0:T(8,128)S(1)} all-to-all(f32[2,128,8,128]{3,2,1,0:T(8,128)S(1)} %bitcast.24), channel_id=1, replica_groups=mesh['y'=8,'xh'=4,'z'=8,'xl'=2,'c'=2] {'c'}, dimensions={0} | all-to-all | bytes 2097152 | tf_op jit(solution)/shard_map/all_to_all | solution.py:26
  53.2 3.2 %collective-permute-done.1.refs_1_.below_tail = f32[4,160,128]{2,1,0:T(8,128)S(1)} collective-permute-done((f32[4,160,128]{2,1,0:T(8,128)S(1)}, f32[4,160,128]{2,1,0:T(8,128)S(1)}, u32[]{:S(2)}, u32[]{:S(2)}) %collective-permute-start.1) | collective-permute-done | bytes 327712 | tf_op jit(solution)/shard_map/ppermute | solution.py:22
  56.4 1.5 shard_map.18
  57.9 4.6 %all_to_all.46 = f32[2,128,8,128]{3,2,1,0:T(8,128)S(1)} all-to-all(f32[2,128,8,128]{3,2,1,0:T(8,128)S(1)} %bitcast.23), channel_id=1, replica_groups=mesh['y'=8,'xh'=4,'z'=8,'xl'=2,'c'=2] {'c'}, dimensions={0} | all-to-all | bytes 2097152 | tf_op jit(solution)/shard_map/all_to_all | solution.py:26
  62.7 59.5 %all_to_all.47 = f32[64,4,8,128]{3,2,1,0:T(8,128)S(1)} all-to-all(f32[64,4,8,128]{3,2,1,0:T(8,128)S(1)} %pad_maximum_fusion), channel_id=1, replica_groups=mesh['y'=8,'xh'=4,'z'=8,'xl'=2,'c'=2] {'xh','z','xl'}, dimensions={0} | all-to-all | bytes 2097152 | tf_op jit(solution)/shard_map/all_to_all | solution.py:26
  123.4 7.5 %all-to-all-start.5 = ((f32[64,4,8,128]{3,2,1,0:T(8,128)}), f32[64,4,8,128]{3,2,1,0:T(8,128)S(1)}, u32[]{:S(2)}, u32[]{:S(2)}) async-start(f32[64,4,8,128]{3,2,1,0:T(8,128)} %broadcast_in_dim.6), calls=%async_computation.5 | async-start | bytes 2097152 | tf_op jit(solution)/shard_map/all_to_all | solution.py:26
  130.9 2.0 collective-permute-start.2
  133.0 26.2 %all-to-all-done.5 = f32[64,4,8,128]{3,2,1,0:T(8,128)S(1)} async-done(((f32[64,4,8,128]{3,2,1,0:T(8,128)}), f32[64,4,8,128]{3,2,1,0:T(8,128)S(1)}, u32[]{:S(2)}, u32[]{:S(2)}) %all-to-all-start.5) | async-done | bytes 1048608 | tf_op jit(solution)/shard_map/all_to_all | solution.py:26
  159.2 2.0 collective-permute-start.4
  161.3 2.4 %collective-permute-start.3 = (f32[4,160,128]{2,1,0:T(8,128)S(1)}, f32[4,160,128]{2,1,0:T(8,128)S(1)}, u32[]{:S(2)}, u32[]{:S(2)}) collective-permute-start(f32[4,160,128]{2,1,0:T(8,128)S(1)} %all-to-all-done.1.row_tail), channel_id=1, source_target_pairs={{0,896},{128,0},{256,128},{384,256},{512,384},{640,512},{768,640},... | collective-permute-start | bytes 983048 | tf_op jit(solution)/shard_map/ppermute | solution.py:22
  163.9 5.4 %all_to_all.48.units_ref = f32[2,64,4,8,128]{4,3,2,1,0:T(8,128)S(1)} all-to-all(f32[2,64,4,8,128]{4,3,2,1,0:T(8,128)S(1)} %broadcast_in_dim.7), channel_id=1, replica_groups=mesh['y'=8,'xh'=4,'z'=8,'xl'=2,'c'=2] {'c'}, dimensions={0} | all-to-all | bytes 4194304 | tf_op jit(solution)/shard_map/all_to_all | solution.py:26
  169.3 2.9 %shard_map.19.part_ref = f32[4,160,384]{2,1,0:T(8,128)S(1)} custom-call(f32[4,160,256]{2,1,0:T(8,128)S(1)} %all-to-all-done.row_head, f32[4,160,128]{2,1,0:T(8,128)S(1)} %all-to-all-done.1.row_tail, f32[4,160,256]{2,1,0:T(8,128)S(1)} %collective-permute-done.refs_0_.below_head, f32[4,160,128]{2,1,0:T(8,128)S(1)} %collective-permute-done.1.refs_1_.below_tail, ...), custom_call_target="tpu_custom_call" | custom-call | tf_op jit(solution)/shard_map/pallas_call | solution.py:51
  172.3 5.3 %collective-permute-done.4 = f32[64,2,8,128]{3,2,1,0:T(8,128)S(1)} collective-permute-done((f32[64,2,8,128]{3,2,1,0:T(8,128)S(1)}, f32[64,2,8,128]{3,2,1,0:T(8,128)S(1)}, u32[]{:S(2)}, u32[]{:S(2)}) %collective-permute-start.4) | collective-permute-done | bytes 524320 | tf_op jit(solution)/shard_map/ppermute | solution.py:22
  178.6 3.6 %all-to-all-start.7 = ((f32[2,64,2,8,128]{4,3,2,1,0:T(8,128)}), f32[2,64,2,8,128]{4,3,2,1,0:T(8,128)S(1)}, u32[]{:S(2)}, u32[]{:S(2)}) async-start(f32[2,64,2,8,128]{4,3,2,1,0:T(8,128)} %broadcast_in_dim.8), calls=%async_computation.7 | async-start | bytes 2097152 | tf_op jit(solution)/shard_map/all_to_all | solution.py:26
  182.3 2.1 all-to-all-done.7.units_ref
  184.3 2.6 %shard_map.20 = f32[4,160,384]{2,1,0:T(8,128)S(1)} custom-call(f32[4,160,384]{2,1,0:T(8,128)S(1)} %shard_map.19.part_ref, f32[4,160,256]{2,1,0:T(8,128)} %collective-permute-done.2.above_head, f32[4,160,128]{2,1,0:T(8,128)S(1)} %collective-permute-done.3.above_tail, f32[2,64,2,8,128]{4,3,2,1,0:T(8,128)S(1)} %all-to-all-done.7.units_ref), custom_call_target="tpu_custom_call" | custom-call | tf_op jit(solution)/shard_map/pallas_call | solution.py:51
  186.9 32.7 %all_to_all.49 = f32[4,160,384]{2,1,0:T(8,128)S(1)} all-to-all(f32[4,160,384]{2,1,0:T(8,128)S(1)} %shard_map.20), channel_id=1, replica_groups=mesh['y'=8,'xh'=4,'z'=8,'xl'=2,'c'=2] {'xh'}, dimensions={0} | all-to-all | bytes 1966080 | tf_op jit(solution)/shard_map/all_to_all | solution.py:26
  (17 shorter events, 7.7 us)
Async XLA Ops:
  2.1 24.8 %all-to-all-start = ((f32[4,160,256]{2,1,0:T(8,128)}), f32[4,160,256]{2,1,0:T(8,128)S(1)}, u32[]{:S(2)}, u32[]{:S(2)}) async-start(f32[4,160,256]{2,1,0:T(8,128)} %pad_maximum_fusion.1), calls=%async_computation | async-start | bytes 1310720 | tf_op jit(solution)/shard_map/all_to_all | solution.py:26
  26.9 15.4 %all-to-all-start.1 = ((f32[4,160,128]{2,1,0:T(8,128)}), f32[4,160,128]{2,1,0:T(8,128)S(1)}, u32[]{:S(2)}, u32[]{:S(2)}) async-start(f32[4,160,128]{2,1,0:T(8,128)} %pad_maximum_fusion.2), calls=%async_computation.1 | async-start | bytes 655360 | tf_op jit(solution)/shard_map/all_to_all | solution.py:26
  31.0 25.4 %collective-permute-start = (f32[4,160,256]{2,1,0:T(8,128)S(1)}, f32[4,160,256]{2,1,0:T(8,128)S(1)}, u32[]{:S(2)}, u32[]{:S(2)}) collective-permute-start(f32[4,160,256]{2,1,0:T(8,128)S(1)} %all-to-all-done.row_head), channel_id=1, source_target_pairs={{0,128},{128,256},{256,384},{384,512},{512,640},{640,768},{768,896... | collective-permute-start | bytes 1966088 | tf_op jit(solution)/shard_map/ppermute | solution.py:22
  42.3 14.2 %collective-permute-start.1 = (f32[4,160,128]{2,1,0:T(8,128)S(1)}, f32[4,160,128]{2,1,0:T(8,128)S(1)}, u32[]{:S(2)}, u32[]{:S(2)}) collective-permute-start(f32[4,160,128]{2,1,0:T(8,128)S(1)} %all-to-all-done.1.row_tail), channel_id=1, source_target_pairs={{0,128},{128,256},{256,384},{384,512},{512,640},{640,768},{768,896... | collective-permute-start | bytes 983048 | tf_op jit(solution)/shard_map/ppermute | solution.py:22
  123.4 35.8 %all-to-all-start.5 = ((f32[64,4,8,128]{3,2,1,0:T(8,128)}), f32[64,4,8,128]{3,2,1,0:T(8,128)S(1)}, u32[]{:S(2)}, u32[]{:S(2)}) async-start(f32[64,4,8,128]{3,2,1,0:T(8,128)} %broadcast_in_dim.6), calls=%async_computation.5 | async-start | bytes 2097152 | tf_op jit(solution)/shard_map/all_to_all | solution.py:26
  130.9 51.3 %collective-permute-start.2 = (f32[4,160,256]{2,1,0:T(8,128)S(1)}, f32[4,160,256]{2,1,0:T(8,128)}, u32[]{:S(2)}, u32[]{:S(2)}) collective-permute-start(f32[4,160,256]{2,1,0:T(8,128)S(1)} %all-to-all-done.row_head), channel_id=1, source_target_pairs={{0,896},{128,0},{256,128},{384,256},{512,384},{640,512},{768,640},... | collective-permute-start | bytes 1966088 | tf_op jit(solution)/shard_map/ppermute | solution.py:22
  159.2 18.4 %collective-permute-start.4 = (f32[64,2,8,128]{3,2,1,0:T(8,128)S(1)}, f32[64,2,8,128]{3,2,1,0:T(8,128)S(1)}, u32[]{:S(2)}, u32[]{:S(2)}) collective-permute-start(f32[64,2,8,128]{3,2,1,0:T(8,128)S(1)} %slice.68), channel_id=1, source_target_pairs={{0,896},{128,0},{256,128},{384,256},{512,384},{640,512},{768,640},... | collective-permute-start | bytes 1572872 | tf_op jit(solution)/shard_map/ppermute | solution.py:22
  161.3 21.0 %collective-permute-start.3 = (f32[4,160,128]{2,1,0:T(8,128)S(1)}, f32[4,160,128]{2,1,0:T(8,128)S(1)}, u32[]{:S(2)}, u32[]{:S(2)}) collective-permute-start(f32[4,160,128]{2,1,0:T(8,128)S(1)} %all-to-all-done.1.row_tail), channel_id=1, source_target_pairs={{0,896},{128,0},{256,128},{384,256},{512,384},{640,512},{768,640},... | collective-permute-start | bytes 983048 | tf_op jit(solution)/shard_map/ppermute | solution.py:22
  178.6 5.7 %all-to-all-start.7 = ((f32[2,64,2,8,128]{4,3,2,1,0:T(8,128)}), f32[2,64,2,8,128]{4,3,2,1,0:T(8,128)S(1)}, u32[]{:S(2)}, u32[]{:S(2)}) async-start(f32[2,64,2,8,128]{4,3,2,1,0:T(8,128)} %broadcast_in_dim.8), calls=%async_computation.7 | async-start | bytes 2097152 | tf_op jit(solution)/shard_map/all_to_all | solution.py:26

commit v4 on v3

--- a/solution.py
+++ b/solution.py
@@ -51,8 +51,54 @@
     return pl.pallas_call(
         kernel,
         out_shape=jax.ShapeDtypeStruct(outs, jnp.float32),
-        compiler_params=pltpu.CompilerParams(vmem_limit_bytes=48 << 20),
+        compiler_params=pltpu.CompilerParams(vmem_limit_bytes=16 << 20),
     )(*operands)
+
+
+def moved(copies, sems):
+    copies = [pltpu.make_async_copy(*copy, sems.at[i]) for i, copy in enumerate(copies)]
+    for copy in copies:
+        copy.start()
+    for copy in copies:
+        copy.wait()
+
+
+def deal_kernel(block, head, tail, sems):
+    split, width = head.shape[2], head.shape[2] + tail.shape[2]
+    copies = [(block.at[:, width * a : width * a + split], head.at[a]) for a in range(GROUPS)]
+    copies += [(block.at[:, width * a + split : width * (a + 1)], tail.at[a]) for a in range(GROUPS)]
+    moved(copies, sems)
+
+
+def deal(block):
+    bands, width = block.shape[0], block.shape[1] // GROUPS
+    split = width // 3 * 2
+    return pl.pallas_call(
+        deal_kernel,
+        out_shape=[
+            jax.ShapeDtypeStruct((GROUPS, bands, size), jnp.float32) for size in (split, width - split)
+        ],
+        in_specs=[pl.BlockSpec(memory_space=pltpu.HBM)],
+        out_specs=[pl.BlockSpec(memory_space=pltpu.VMEM)] * 2,
+        scratch_shapes=[pltpu.SemaphoreType.DMA((2 * GROUPS,))],
+        compiler_params=pltpu.CompilerParams(vmem_limit_bytes=4 << 20),
+    )(block)
+
+
+def collect_kernel(quarters, block, sems):
+    width = quarters.shape[2]
+    moved([(quarters.at[a], block.at[:, width * a : width * (a + 1)]) for a in range(GROUPS)], sems)
+
+
+def collect(quarters):
+    return pl.pallas_call(
+        collect_kernel,
+        out_shape=jax.ShapeDtypeStruct((quarters.shape[1], GROUPS * quarters.shape[2]), jnp.float32),
+        in_specs=[pl.BlockSpec(memory_space=pltpu.VMEM)],
+        out_specs=pl.BlockSpec(memory_space=pltpu.HBM),
+        scratch_shapes=[pltpu.SemaphoreType.DMA((GROUPS,))],
+        compiler_params=pltpu.CompilerParams(vmem_limit_bytes=4 << 20),
+    )(quarters)
 
 
 def joined(head_ref, tail_ref):
@@ -85,7 +131,7 @@
     units_ref[250:] = jnp.zeros((6, ROWS, UNIT), jnp.float32)
 
 
-def strips_of(units_ref, offset):
+def strips_of(units_of):
     half = UNITS // 2
 
     def get(index, count=20):
@@ -94,7 +140,7 @@
         for core in range(2):
             low, high = max(start, half * core) - half * core, min(stop, half * (core + 1)) - half * core
             if low < high:
-                part = units_ref[core, low // 2 : high // 2, offset : offset + 2]
+                part = units_of(core, slice(low // 2, high // 2))
                 parts.append(part.reshape(high - low, ROWS, UNIT))
         value = parts[0] if len(parts) == 1 else jnp.concatenate(parts)
         return value.reshape(count * ROWS, UNIT)
@@ -112,8 +158,8 @@
     row = joined(row_head, row_tail)
     rows = halves(row)
     below = halves(joined(below_head, below_tail))
-    inner = strips_of(units_ref, 0)[::-1]
-    outer = strips_of(units_ref, 2)
+    inner = strips_of(lambda core, pairs: units_ref[core, pairs, 0:2])[::-1]
+    outer = strips_of(lambda core, pairs: units_ref[core, pairs, 2:4])
     fix = []
     for a in range(GROUPS):
         width = bands * (a + 1)
@@ -134,10 +180,16 @@
         out_ref[a] = row[bands * a : bands * (a + 1)] - 0.5 * fix[a]
 
 
-def above_kernel(part_ref, above_head, above_tail, units_ref, out_ref):
+def above_kernel(core_ref, part_ref, above_head, above_tail, own_ref, partner_ref, out_ref):
+    first = core_ref[0] == 0
     bands = part_ref.shape[1]
     above = halves(joined(above_head, above_tail))
-    strips = strips_of(units_ref, 0)
+
+    def units_of(core, pairs):
+        own, partner = own_ref[pairs], partner_ref[pairs]
+        return jnp.where(first, own, partner) if core == 0 else jnp.where(first, partner, own)
+
+    strips = strips_of(units_of)
     fix = [None] * GROUPS
     for b in range(GROUPS):
         back = product(halves(strips[b]), cut(above, slice(bands * b, bands * (b + 1))), TN)
@@ -156,12 +208,10 @@
     bands = orbitals.shape[0]
     points = orbitals.shape[1] * lax.axis_size(("z", "xl", "c"))
     members = lax.axis_size(RING)
-    width = orbitals.shape[1] // GROUPS
-    split = width // 3 * 2
-    pieces = [orbitals[:, width * a : width * (a + 1)] for a in range(GROUPS)]
-    head = exchange(jnp.stack([piece[:, :split] for piece in pieces]), "xh")
+    head, tail = deal(orbitals)
+    head = exchange(head, "xh")
     below_head = passed_along(head, 1)
-    tail = exchange(jnp.stack([piece[:, split:] for piece in pieces]), "xh")
+    tail = exchange(tail, "xh")
     below_tail = passed_along(tail, 1)
     above_head = passed_along(head, -1)
     above_tail = passed_along(tail, -1)
@@ -178,10 +228,17 @@
     share = share.sum(0) / points
     both = spread(share, RING)
     following = passed_along(both[:, 2:], -1)
-    shape = (GROUPS, bands, width)
+    shape = (GROUPS, bands, orbitals.shape[1] // GROUPS)
     part = call(apply_kernel, shape, head, tail, below_head, below_tail, spread(both, "c"))
-    corrected = call(above_kernel, shape, part, above_head, above_tail, spread(following, "c"))
-    return exchange(corrected, "xh").transpose(1, 0, 2).reshape(orbitals.shape)
+    part, following = lax.optimization_barrier((part, following))
+    partner = lax.ppermute(following, "c", [(0, 1), (1, 0)])
+    corrected = pl.pallas_call(
+        above_kernel,
+        out_shape=jax.ShapeDtypeStruct(shape, jnp.float32),
+        in_specs=[pl.BlockSpec(memory_space=pltpu.SMEM)] + [pl.BlockSpec(memory_space=pltpu.VMEM)] * 5,
+        compiler_params=pltpu.CompilerParams(vmem_limit_bytes=16 << 20),
+    )(lax.axis_index("c").reshape(1), part, above_head, above_tail, following, partner)
+    return collect(exchange(corrected, "xh"))
 
 
 def solution(mesh):

time: 221 us -> 229 us (1.036)
  blocking collectives: 107 us -> 166 us
  waiting for transfers between devices: 59.6 us -> 28.7 us
  starting transfers between devices: 38 us -> 21.4 us
  local copies, waits for them, and re-layouts: 5.72 us -> 1.6 us
    all_to_all x5 -> x7, blocking collectives: 107 us -> 166 us  [exchange(): return lax.all_to_all(pieces, axes, 0, 0)]
    all_to_all x4 -> x1, waiting for transfers between devices: 51 us -> 5.76 us  [exchange(): return lax.all_to_all(pieces, axes, 0, 0)]
    all_to_all x4 -> x1, starting transfers between devices: 22 us -> 3.45 us  [exchange(): return lax.all_to_all(pieces, axes, 0, 0)]
    ppermute x5, waiting for transfers between devices: 8.55 us -> 23 us  [passed_along(): lax.ppermute(block, 'y', [(i, (i + distance) % count) for i in range(coun...]
    pallas_call x0 -> x3, Pallas kernels: none -> 4.5 us  [the longest x1 2.59 us: shards(): pl.pallas_call(above_kernel, out_shape=jax.ShapeDtypeStruct(shape, jnp.fl...]
    pallas_call x4 -> x3, Pallas kernels: 8.52 us -> 5.94 us  [call(): pl.pallas_call(kernel, out_shape=jax.ShapeDtypeStruct(outs, jnp.float32),...]
  transfers between devices with their start and end apart: 9 -> 7, of which waited for: 6 -> 4; matrix products, arithmetic and copies ran while one was open for 1% -> 0% of each run, Pallas kernels for 2% -> 2%
where the time goes in v4:
time: 229 us
  blocking collectives  166 us (72%)
  waiting for transfers between devices  28.7 us (13%)
  starting transfers between devices  21.4 us (9%)
  Pallas kernels  10.4 us (5%)
    all_to_all x7, blocking collectives, exchange(): return lax.all_to_all(pieces, axes, 0, 0)  166 us
    ppermute x5, waiting for transfers between devices, passed_along(): lax.ppermute(block, 'y', [(i, (i + distance) % count) for i in range(coun...  23 us
    ppermute x5, starting transfers between devices, passed_along(): lax.ppermute(block, 'y', [(i, (i + distance) % count) for i in range(coun...  16 us
    pallas_call x3, Pallas kernels, call(): pl.pallas_call(kernel, out_shape=jax.ShapeDtypeStruct(outs, jnp.float32),...  5.94 us
    all_to_all x1, waiting for transfers between devices, exchange(): return lax.all_to_all(pieces, axes, 0, 0)  5.76 us
  transfers between devices with their start and end apart: 7, of which 4 were waited for; matrix products, arithmetic and copies ran while one was open for 0% of the time, Pallas kernels for 2%

profile of v4, /device:TPU:48, one launch (start us, length us, event | category | flops | bytes accessed | tf_op | source)
XLA Modules:
  0.0 228.6 jit_solution(13436771162193919186)
XLA Ops:
  0.0 1.2 copy-done
  2.2 25.6 %all_to_all.40.row_head = f32[4,160,256]{2,1,0:T(8,128)S(1)} all-to-all(f32[4,160,256]{2,1,0:T(8,128)S(1)} %get-tuple-element.12), channel_id=1, replica_groups=mesh['y'=8,'xh'=4,'z'=8,'xl'=2,'c'=2] {'xh'}, dimensions={0} | all-to-all | bytes 1310720 | tf_op jit(solution)/shard_map/all_to_all | solution.py:26
  27.8 3.5 %all-to-all-start.1 = ((f32[4,160,128]{2,1,0:T(8,128)}), f32[4,160,128]{2,1,0:T(8,128)S(1)}, u32[]{:S(2)}, u32[]{:S(2)}) async-start(f32[4,160,128]{2,1,0:T(8,128)} %get-tuple-element.13), calls=%async_computation.1 | async-start | bytes 655360 | tf_op jit(solution)/shard_map/all_to_all | solution.py:26
  31.3 4.8 %collective-permute-start = (f32[4,160,256]{2,1,0:T(8,128)S(1)}, f32[4,160,256]{2,1,0:T(8,128)S(1)}, u32[]{:S(2)}, u32[]{:S(2)}) collective-permute-start(f32[4,160,256]{2,1,0:T(8,128)S(1)} %all_to_all.40.row_head), channel_id=1, source_target_pairs={{0,128},{128,256},{256,384},{384,512},{512,640},{640,768},{768,896... | collective-permute-start | bytes 1966088 | tf_op jit(solution)/shard_map/ppermute | solution.py:22
  36.1 5.8 %all-to-all-done.1.row_tail = f32[4,160,128]{2,1,0:T(8,128)S(1)} async-done(((f32[4,160,128]{2,1,0:T(8,128)}), f32[4,160,128]{2,1,0:T(8,128)S(1)}, u32[]{:S(2)}, u32[]{:S(2)}) %all-to-all-start.1) | async-done | bytes 327712 | tf_op jit(solution)/shard_map/all_to_all | solution.py:26
  41.8 4.8 %collective-permute-start.1 = (f32[4,160,128]{2,1,0:T(8,128)S(1)}, f32[4,160,128]{2,1,0:T(8,128)S(1)}, u32[]{:S(2)}, u32[]{:S(2)}) collective-permute-start(f32[4,160,128]{2,1,0:T(8,128)S(1)} %all-to-all-done.1.row_tail), channel_id=1, source_target_pairs={{0,128},{128,256},{256,384},{384,512},{512,640},{640,768},{768,896... | collective-permute-start | bytes 983048 | tf_op jit(solution)/shard_map/ppermute | solution.py:22
  46.6 1.5 shard_map.18
  48.1 4.6 %all_to_all.41 = f32[2,128,8,128]{3,2,1,0:T(8,128)S(1)} all-to-all(f32[2,128,8,128]{3,2,1,0:T(8,128)S(1)} %bitcast.6), channel_id=1, replica_groups=mesh['y'=8,'xh'=4,'z'=8,'xl'=2,'c'=2] {'c'}, dimensions={0} | all-to-all | bytes 2097152 | tf_op jit(solution)/shard_map/all_to_all | solution.py:26
  52.8 3.5 %collective-permute-done.1.refs_1_.below_tail = f32[4,160,128]{2,1,0:T(8,128)S(1)} collective-permute-done((f32[4,160,128]{2,1,0:T(8,128)S(1)}, f32[4,160,128]{2,1,0:T(8,128)S(1)}, u32[]{:S(2)}, u32[]{:S(2)}) %collective-permute-start.1) | collective-permute-done | bytes 327712 | tf_op jit(solution)/shard_map/ppermute | solution.py:22
  56.3 1.5 shard_map.19
  57.8 4.6 %all_to_all.42 = f32[2,128,8,128]{3,2,1,0:T(8,128)S(1)} all-to-all(f32[2,128,8,128]{3,2,1,0:T(8,128)S(1)} %bitcast.5), channel_id=1, replica_groups=mesh['y'=8,'xh'=4,'z'=8,'xl'=2,'c'=2] {'c'}, dimensions={0} | all-to-all | bytes 2097152 | tf_op jit(solution)/shard_map/all_to_all | solution.py:26
  62.6 59.5 %all_to_all.43 = f32[64,4,8,128]{3,2,1,0:T(8,128)S(1)} all-to-all(f32[64,4,8,128]{3,2,1,0:T(8,128)S(1)} %pad_maximum_fusion), channel_id=1, replica_groups=mesh['y'=8,'xh'=4,'z'=8,'xl'=2,'c'=2] {'xh','z','xl'}, dimensions={0} | all-to-all | bytes 2097152 | tf_op jit(solution)/shard_map/all_to_all | solution.py:26
  122.3 35.6 %all_to_all.44 = f32[64,4,8,128]{3,2,1,0:T(8,128)S(1)} all-to-all(f32[64,4,8,128]{3,2,1,0:T(8,128)S(1)} %broadcast_in_dim.4), channel_id=1, replica_groups=mesh['y'=8,'xh'=4,'z'=8,'xl'=2,'c'=2] {'xh','z','xl'}, dimensions={0} | all-to-all | bytes 2097152 | tf_op jit(solution)/shard_map/all_to_all | solution.py:26
  158.0 2.1 collective-permute-start.2
  160.1 2.4 %collective-permute-start.3 = (f32[4,160,256]{2,1,0:T(8,128)S(1)}, f32[4,160,256]{2,1,0:T(8,128)}, u32[]{:S(2)}, u32[]{:S(2)}) collective-permute-start(f32[4,160,256]{2,1,0:T(8,128)S(1)} %all_to_all.40.row_head), channel_id=1, source_target_pairs={{0,896},{128,0},{256,128},{384,256},{512,384},{640,512},{768,640},... | collective-permute-start | bytes 1966088 | tf_op jit(solution)/shard_map/ppermute | solution.py:22
  162.7 5.4 %all_to_all.45.units_ref = f32[2,64,4,8,128]{4,3,2,1,0:T(8,128)S(1)} all-to-all(f32[2,64,4,8,128]{4,3,2,1,0:T(8,128)S(1)} %broadcast_in_dim.5), channel_id=1, replica_groups=mesh['y'=8,'xh'=4,'z'=8,'xl'=2,'c'=2] {'c'}, dimensions={0} | all-to-all | bytes 4194304 | tf_op jit(solution)/shard_map/all_to_all | solution.py:26
  168.2 2.9 %shard_map.20.part_ref = f32[4,160,384]{2,1,0:T(8,128)S(1)} custom-call(f32[4,160,256]{2,1,0:T(8,128)S(1)} %all_to_all.40.row_head, f32[4,160,128]{2,1,0:T(8,128)S(1)} %all-to-all-done.1.row_tail, f32[4,160,256]{2,1,0:T(8,128)S(1)} %collective-permute-done.refs_0_.below_head, f32[4,160,128]{2,1,0:T(8,128)S(1)} %collective-permute-done.1.refs_1_.below_tail, ...), custom_call_target="tpu_custom_call" | custom-call | tf_op jit(solution)/shard_map/pallas_call | solution.py:51
  171.1 5.3 %collective-permute-done.2.own_ref = f32[64,2,8,128]{3,2,1,0:T(8,128)S(1)} collective-permute-done((f32[64,2,8,128]{3,2,1,0:T(8,128)S(1)}, f32[64,2,8,128]{3,2,1,0:T(8,128)S(1)}, u32[]{:S(2)}, u32[]{:S(2)}) %collective-permute-start.2) | collective-permute-done | bytes 524320 | tf_op jit(solution)/shard_map/ppermute | solution.py:22
  176.4 1.9 collective-permute-start.5
  178.3 1.9 collective-permute-start.4
  180.2 14.2 %collective-permute-done.4.above_tail = f32[4,160,128]{2,1,0:T(8,128)S(1)} collective-permute-done((f32[4,160,128]{2,1,0:T(8,128)S(1)}, f32[4,160,128]{2,1,0:T(8,128)S(1)}, u32[]{:S(2)}, u32[]{:S(2)}) %collective-permute-start.4) | collective-permute-done | bytes 327712 | tf_op jit(solution)/shard_map/ppermute | solution.py:22
  194.4 2.6 %shard_map.21 = f32[4,160,384]{2,1,0:T(8,128)S(1)} custom-call(s32[1]{0:T(128)} %bitcast.core_ref, f32[4,160,384]{2,1,0:T(8,128)S(1)} %shard_map.20.part_ref, f32[4,160,256]{2,1,0:T(8,128)} %collective-permute-done.3.above_head, f32[4,160,128]{2,1,0:T(8,128)S(1)} %collective-permute-done.4.above_tail, f32[64,2,8,128]{3,2,1,0:T(8,128)S(1)} %collective-permute-done.2.own_ref, ...), custom_call_target="tpu_custom_call" | custom-call | tf_op jit(solution)/shard_map/pallas_call | solution.py:235
  197.0 30.6 %all_to_all.46.quarters = f32[4,160,384]{2,1,0:T(8,128)S(1)} all-to-all(f32[4,160,384]{2,1,0:T(8,128)S(1)} %shard_map.21), channel_id=1, replica_groups=mesh['y'=8,'xh'=4,'z'=8,'xl'=2,'c'=2] {'xh'}, dimensions={0} | all-to-all | bytes 1966080 | tf_op jit(solution)/shard_map/all_to_all | solution.py:26
  227.6 1.0 shard_map.22
  (13 shorter events, 1.7 us)
Async XLA Ops:
  0.0 1.2 copy-start
  27.8 14.0 %all-to-all-start.1 = ((f32[4,160,128]{2,1,0:T(8,128)}), f32[4,160,128]{2,1,0:T(8,128)S(1)}, u32[]{:S(2)}, u32[]{:S(2)}) async-start(f32[4,160,128]{2,1,0:T(8,128)} %get-tuple-element.13), calls=%async_computation.1 | async-start | bytes 655360 | tf_op jit(solution)/shard_map/all_to_all | solution.py:26
  31.3 25.0 %collective-permute-start = (f32[4,160,256]{2,1,0:T(8,128)S(1)}, f32[4,160,256]{2,1,0:T(8,128)S(1)}, u32[]{:S(2)}, u32[]{:S(2)}) collective-permute-start(f32[4,160,256]{2,1,0:T(8,128)S(1)} %all_to_all.40.row_head), channel_id=1, source_target_pairs={{0,128},{128,256},{256,384},{384,512},{512,640},{640,768},{768,896... | collective-permute-start | bytes 1966088 | tf_op jit(solution)/shard_map/ppermute | solution.py:22
  41.8 14.5 %collective-permute-start.1 = (f32[4,160,128]{2,1,0:T(8,128)S(1)}, f32[4,160,128]{2,1,0:T(8,128)S(1)}, u32[]{:S(2)}, u32[]{:S(2)}) collective-permute-start(f32[4,160,128]{2,1,0:T(8,128)S(1)} %all-to-all-done.1.row_tail), channel_id=1, source_target_pairs={{0,128},{128,256},{256,384},{384,512},{512,640},{640,768},{768,896... | collective-permute-start | bytes 983048 | tf_op jit(solution)/shard_map/ppermute | solution.py:22
  158.0 18.4 %collective-permute-start.2 = (f32[64,2,8,128]{3,2,1,0:T(8,128)S(1)}, f32[64,2,8,128]{3,2,1,0:T(8,128)S(1)}, u32[]{:S(2)}, u32[]{:S(2)}) collective-permute-start(f32[64,2,8,128]{3,2,1,0:T(8,128)S(1)} %slice.24), channel_id=1, source_target_pairs={{0,896},{128,0},{256,128},{384,256},{512,384},{640,512},{768,640},... | collective-permute-start | bytes 1572872 | tf_op jit(solution)/shard_map/ppermute | solution.py:22
  160.1 34.3 %collective-permute-start.3 = (f32[4,160,256]{2,1,0:T(8,128)S(1)}, f32[4,160,256]{2,1,0:T(8,128)}, u32[]{:S(2)}, u32[]{:S(2)}) collective-permute-start(f32[4,160,256]{2,1,0:T(8,128)S(1)} %all_to_all.40.row_head), channel_id=1, source_target_pairs={{0,896},{128,0},{256,128},{384,256},{512,384},{640,512},{768,640},... | collective-permute-start | bytes 1966088 | tf_op jit(solution)/shard_map/ppermute | solution.py:22
  176.4 18.1 %collective-permute-start.5 = (f32[64,2,8,128]{3,2,1,0:T(8,128)S(1)}, f32[64,2,8,128]{3,2,1,0:T(8,128)S(1)}, u32[]{:S(2)}, u32[]{:S(2)}) collective-permute-start(f32[64,2,8,128]{3,2,1,0:T(8,128)S(1)} %collective-permute-done.2.own_ref), channel_id=1, source_target_pairs={{0,1},{1,0},{2,3},{3,2},{4,5},{5,4},{6,7},{7,6},{8,9},{9,8},{10,11... | collective-permute-start | bytes 1572872 | tf_op jit(solution)/shard_map/ppermute | solution.py:234
  178.3 16.1 %collective-permute-start.4 = (f32[4,160,128]{2,1,0:T(8,128)S(1)}, f32[4,160,128]{2,1,0:T(8,128)S(1)}, u32[]{:S(2)}, u32[]{:S(2)}) collective-permute-start(f32[4,160,128]{2,1,0:T(8,128)S(1)} %all-to-all-done.1.row_tail), channel_id=1, source_target_pairs={{0,896},{128,0},{256,128},{384,256},{512,384},{640,512},{768,640},... | collective-permute-start | bytes 983048 | tf_op jit(solution)/shard_map/ppermute | solution.py:22

commit v5 on v4

--- a/solution.py
+++ b/solution.py
@@ -85,20 +85,22 @@
     )(block)
 
 
-def collect_kernel(quarters, block, sems):
-    width = quarters.shape[2]
-    moved([(quarters.at[a], block.at[:, width * a : width * (a + 1)]) for a in range(GROUPS)], sems)
-
-
-def collect(quarters):
+def collect_kernel(head, tail, block, sems):
+    split, width = head.shape[2], head.shape[2] + tail.shape[2]
+    copies = [(head.at[a], block.at[:, width * a : width * a + split]) for a in range(GROUPS)]
+    copies += [(tail.at[a], block.at[:, width * a + split : width * (a + 1)]) for a in range(GROUPS)]
+    moved(copies, sems)
+
+
+def collect(head, tail):
     return pl.pallas_call(
         collect_kernel,
-        out_shape=jax.ShapeDtypeStruct((quarters.shape[1], GROUPS * quarters.shape[2]), jnp.float32),
-        in_specs=[pl.BlockSpec(memory_space=pltpu.VMEM)],
+        out_shape=jax.ShapeDtypeStruct((head.shape[1], GROUPS * (head.shape[2] + tail.shape[2])), jnp.float32),
+        in_specs=[pl.BlockSpec(memory_space=pltpu.VMEM)] * 2,
         out_specs=pl.BlockSpec(memory_space=pltpu.HBM),
-        scratch_shapes=[pltpu.SemaphoreType.DMA((GROUPS,))],
+        scratch_shapes=[pltpu.SemaphoreType.DMA((2 * GROUPS,))],
         compiler_params=pltpu.CompilerParams(vmem_limit_bytes=4 << 20),
-    )(quarters)
+    )(head, tail)
 
 
 def joined(head_ref, tail_ref):
@@ -180,8 +182,9 @@
         out_ref[a] = row[bands * a : bands * (a + 1)] - 0.5 * fix[a]
 
 
-def above_kernel(core_ref, part_ref, above_head, above_tail, own_ref, partner_ref, out_ref):
+def above_kernel(core_ref, part_ref, above_head, above_tail, own_ref, partner_ref, head_out, tail_out):
     first = core_ref[0] == 0
+    split = head_out.shape[2]
     bands = part_ref.shape[1]
     above = halves(joined(above_head, above_tail))
 
@@ -197,7 +200,9 @@
             term = back[bands * (a - b) : bands * (a - b + 1)]
             fix[a] = term if b == 0 else fix[a] + term
     for a in range(GROUPS):
-        out_ref[a] = part_ref[a] - 0.5 * fix[a]
+        corrected = part_ref[a] - 0.5 * fix[a]
+        head_out[a] = corrected[:, :split]
+        tail_out[a] = corrected[:, split:]
 
 
 INNER = [(3, 0, 4), (2, 0, 3), (1, 0, 2), (0, 0, 1)]
@@ -208,7 +213,7 @@
     bands = orbitals.shape[0]
     points = orbitals.shape[1] * lax.axis_size(("z", "xl", "c"))
     members = lax.axis_size(RING)
-    head, tail = deal(orbitals)
+    head, tail = deal(pltpu.with_memory_space_constraint(orbitals, pltpu.HBM))
     head = exchange(head, "xh")
     below_head = passed_along(head, 1)
     tail = exchange(tail, "xh")
@@ -232,13 +237,13 @@
     part = call(apply_kernel, shape, head, tail, below_head, below_tail, spread(both, "c"))
     part, following = lax.optimization_barrier((part, following))
     partner = lax.ppermute(following, "c", [(0, 1), (1, 0)])
-    corrected = pl.pallas_call(
+    head, tail = pl.pallas_call(
         above_kernel,
-        out_shape=jax.ShapeDtypeStruct(shape, jnp.float32),
+        out_shape=[jax.ShapeDtypeStruct(chunk.shape, jnp.float32) for chunk in (head, tail)],
         in_specs=[pl.BlockSpec(memory_space=pltpu.SMEM)] + [pl.BlockSpec(memory_space=pltpu.VMEM)] * 5,
         compiler_params=pltpu.CompilerParams(vmem_limit_bytes=16 << 20),
     )(lax.axis_index("c").reshape(1), part, above_head, above_tail, following, partner)
-    return collect(exchange(corrected, "xh"))
+    return collect(exchange(head, "xh"), exchange(tail, "xh"))
 
 
 def solution(mesh):

time: 229 us -> 234 us (1.022)
  blocking collectives: 166 us -> 170 us
    all_to_all x7 -> x8, blocking collectives: 166 us -> 170 us  [exchange(): return lax.all_to_all(pieces, axes, 0, 0)]
where the time goes in v5:
time: 234 us; the launch traced here: 233 us
  blocking collectives  170 us (73%)
  waiting for transfers between devices  28.7 us (12%)
  starting transfers between devices  21.4 us (9%)
  Pallas kernels  11.6 us (5%)
    all_to_all x8, blocking collectives, exchange(): return lax.all_to_all(pieces, axes, 0, 0)  170 us
    ppermute x5, waiting for transfers between devices, passed_along(): lax.ppermute(block, 'y', [(i, (i + distance) % count) for i in range(coun...  22.9 us
    ppermute x5, starting transfers between devices, passed_along(): lax.ppermute(block, 'y', [(i, (i + distance) % count) for i in range(coun...  16 us
    pallas_call x3, Pallas kernels, call(): pl.pallas_call(kernel, out_shape=jax.ShapeDtypeStruct(outs, jnp.float32),...  5.94 us
    all_to_all x1, waiting for transfers between devices, exchange(): return lax.all_to_all(pieces, axes, 0, 0)  5.76 us
  transfers between devices with their start and end apart: 7, of which 4 were waited for; matrix products, arithmetic and copies ran while one was open for 0% of the time, Pallas kernels for 2%

profile of v5, /device:TPU:48, one launch (start us, length us, event | category | flops | bytes accessed | tf_op | source)
XLA Modules:
  0.0 233.1 jit_solution(6362289562284110102)
XLA Ops:
  0.0 2.1 shard_map.17
  2.1 25.6 %all_to_all.45.row_head = f32[4,160,256]{2,1,0:T(8,128)S(1)} all-to-all(f32[4,160,256]{2,1,0:T(8,128)S(1)} %get-tuple-element.14), channel_id=1, replica_groups=mesh['y'=8,'xh'=4,'z'=8,'xl'=2,'c'=2] {'xh'}, dimensions={0} | all-to-all | bytes 1310720 | tf_op jit(solution)/shard_map/all_to_all | solution.py:26
  27.7 3.5 %all-to-all-start.1 = ((f32[4,160,128]{2,1,0:T(8,128)}), f32[4,160,128]{2,1,0:T(8,128)S(1)}, u32[]{:S(2)}, u32[]{:S(2)}) async-start(f32[4,160,128]{2,1,0:T(8,128)} %get-tuple-element.15), calls=%async_computation.1 | async-start | bytes 655360 | tf_op jit(solution)/shard_map/all_to_all | solution.py:26
  31.2 4.8 %collective-permute-start = (f32[4,160,256]{2,1,0:T(8,128)S(1)}, f32[4,160,256]{2,1,0:T(8,128)S(1)}, u32[]{:S(2)}, u32[]{:S(2)}) collective-permute-start(f32[4,160,256]{2,1,0:T(8,128)S(1)} %all_to_all.45.row_head), channel_id=1, source_target_pairs={{0,128},{128,256},{256,384},{384,512},{512,640},{640,768},{768,896... | collective-permute-start | bytes 1966088 | tf_op jit(solution)/shard_map/ppermute | solution.py:22
  36.0 5.8 %all-to-all-done.1.row_tail = f32[4,160,128]{2,1,0:T(8,128)S(1)} async-done(((f32[4,160,128]{2,1,0:T(8,128)}), f32[4,160,128]{2,1,0:T(8,128)S(1)}, u32[]{:S(2)}, u32[]{:S(2)}) %all-to-all-start.1) | async-done | bytes 327712 | tf_op jit(solution)/shard_map/all_to_all | solution.py:26
  41.8 4.8 %collective-permute-start.1 = (f32[4,160,128]{2,1,0:T(8,128)S(1)}, f32[4,160,128]{2,1,0:T(8,128)S(1)}, u32[]{:S(2)}, u32[]{:S(2)}) collective-permute-start(f32[4,160,128]{2,1,0:T(8,128)S(1)} %all-to-all-done.1.row_tail), channel_id=1, source_target_pairs={{0,128},{128,256},{256,384},{384,512},{512,640},{640,768},{768,896... | collective-permute-start | bytes 983048 | tf_op jit(solution)/shard_map/ppermute | solution.py:22
  46.6 1.5 shard_map.18
  48.1 4.6 %all_to_all.46 = f32[2,128,8,128]{3,2,1,0:T(8,128)S(1)} all-to-all(f32[2,128,8,128]{3,2,1,0:T(8,128)S(1)} %bitcast.6), channel_id=1, replica_groups=mesh['y'=8,'xh'=4,'z'=8,'xl'=2,'c'=2] {'c'}, dimensions={0} | all-to-all | bytes 2097152 | tf_op jit(solution)/shard_map/all_to_all | solution.py:26
  52.7 3.5 %collective-permute-done.1.refs_1_.below_tail = f32[4,160,128]{2,1,0:T(8,128)S(1)} collective-permute-done((f32[4,160,128]{2,1,0:T(8,128)S(1)}, f32[4,160,128]{2,1,0:T(8,128)S(1)}, u32[]{:S(2)}, u32[]{:S(2)}) %collective-permute-start.1) | collective-permute-done | bytes 327712 | tf_op jit(solution)/shard_map/ppermute | solution.py:22
  56.2 1.5 shard_map.19
  57.7 4.6 %all_to_all.47 = f32[2,128,8,128]{3,2,1,0:T(8,128)S(1)} all-to-all(f32[2,128,8,128]{3,2,1,0:T(8,128)S(1)} %bitcast.5), channel_id=1, replica_groups=mesh['y'=8,'xh'=4,'z'=8,'xl'=2,'c'=2] {'c'}, dimensions={0} | all-to-all | bytes 2097152 | tf_op jit(solution)/shard_map/all_to_all | solution.py:26
  62.5 59.5 %all_to_all.48 = f32[64,4,8,128]{3,2,1,0:T(8,128)S(1)} all-to-all(f32[64,4,8,128]{3,2,1,0:T(8,128)S(1)} %pad_maximum_fusion), channel_id=1, replica_groups=mesh['y'=8,'xh'=4,'z'=8,'xl'=2,'c'=2] {'xh','z','xl'}, dimensions={0} | all-to-all | bytes 2097152 | tf_op jit(solution)/shard_map/all_to_all | solution.py:26
  122.2 35.6 %all_to_all.49 = f32[64,4,8,128]{3,2,1,0:T(8,128)S(1)} all-to-all(f32[64,4,8,128]{3,2,1,0:T(8,128)S(1)} %broadcast_in_dim.4), channel_id=1, replica_groups=mesh['y'=8,'xh'=4,'z'=8,'xl'=2,'c'=2] {'xh','z','xl'}, dimensions={0} | all-to-all | bytes 2097152 | tf_op jit(solution)/shard_map/all_to_all | solution.py:26
  157.9 2.1 collective-permute-start.2
  160.0 2.4 %collective-permute-start.3 = (f32[4,160,256]{2,1,0:T(8,128)S(1)}, f32[4,160,256]{2,1,0:T(8,128)}, u32[]{:S(2)}, u32[]{:S(2)}) collective-permute-start(f32[4,160,256]{2,1,0:T(8,128)S(1)} %all_to_all.45.row_head), channel_id=1, source_target_pairs={{0,896},{128,0},{256,128},{384,256},{512,384},{640,512},{768,640},... | collective-permute-start | bytes 1966088 | tf_op jit(solution)/shard_map/ppermute | solution.py:22
  162.7 5.4 %all_to_all.50.units_ref = f32[2,64,4,8,128]{4,3,2,1,0:T(8,128)S(1)} all-to-all(f32[2,64,4,8,128]{4,3,2,1,0:T(8,128)S(1)} %broadcast_in_dim.5), channel_id=1, replica_groups=mesh['y'=8,'xh'=4,'z'=8,'xl'=2,'c'=2] {'c'}, dimensions={0} | all-to-all | bytes 4194304 | tf_op jit(solution)/shard_map/all_to_all | solution.py:26
  168.1 2.9 %shard_map.20.part_ref = f32[4,160,384]{2,1,0:T(8,128)S(1)} custom-call(f32[4,160,256]{2,1,0:T(8,128)S(1)} %all_to_all.45.row_head, f32[4,160,128]{2,1,0:T(8,128)S(1)} %all-to-all-done.1.row_tail, f32[4,160,256]{2,1,0:T(8,128)S(1)} %collective-permute-done.refs_0_.below_head, f32[4,160,128]{2,1,0:T(8,128)S(1)} %collective-permute-done.1.refs_1_.below_tail, ...), custom_call_target="tpu_custom_call" | custom-call | tf_op jit(solution)/shard_map/pallas_call | solution.py:51
  171.0 5.2 %collective-permute-done.2.own_ref = f32[64,2,8,128]{3,2,1,0:T(8,128)S(1)} collective-permute-done((f32[64,2,8,128]{3,2,1,0:T(8,128)S(1)}, f32[64,2,8,128]{3,2,1,0:T(8,128)S(1)}, u32[]{:S(2)}, u32[]{:S(2)}) %collective-permute-start.2) | collective-permute-done | bytes 524320 | tf_op jit(solution)/shard_map/ppermute | solution.py:22
  176.2 1.9 collective-permute-start.5
  178.2 1.9 collective-permute-start.4
  180.1 14.2 %collective-permute-done.4.above_tail = f32[4,160,128]{2,1,0:T(8,128)S(1)} collective-permute-done((f32[4,160,128]{2,1,0:T(8,128)S(1)}, f32[4,160,128]{2,1,0:T(8,128)S(1)}, u32[]{:S(2)}, u32[]{:S(2)}) %collective-permute-start.4) | collective-permute-done | bytes 327712 | tf_op jit(solution)/shard_map/ppermute | solution.py:22
  194.3 2.6 %shard_map.21 = (f32[4,160,256]{2,1,0:T(8,128)S(1)}, f32[4,160,128]{2,1,0:T(8,128)S(1)}) custom-call(s32[1]{0:T(128)} %bitcast.core_ref, f32[4,160,384]{2,1,0:T(8,128)S(1)} %shard_map.20.part_ref, f32[4,160,256]{2,1,0:T(8,128)} %collective-permute-done.3.above_head, f32[4,160,128]{2,1,0:T(8,128)S(1)} %collective-permute-done.4.above_tail, ...), custom_call_target="tpu_custom_call" | custom-call | tf_op jit(solution)/shard_map/pallas_call | solution.py:240
  196.9 16.5 %all_to_all.51.tail = f32[4,160,128]{2,1,0:T(8,128)S(1)} all-to-all(f32[4,160,128]{2,1,0:T(8,128)S(1)} %get-tuple-element.22), channel_id=1, replica_groups=mesh['y'=8,'xh'=4,'z'=8,'xl'=2,'c'=2] {'xh'}, dimensions={0} | all-to-all | bytes 655360 | tf_op jit(solution)/shard_map/all_to_all | solution.py:26
  213.4 18.7 %all_to_all.52.head = f32[4,160,256]{2,1,0:T(8,128)S(1)} all-to-all(f32[4,160,256]{2,1,0:T(8,128)S(1)} %get-tuple-element.21), channel_id=1, replica_groups=mesh['y'=8,'xh'=4,'z'=8,'xl'=2,'c'=2] {'xh'}, dimensions={0} | all-to-all | bytes 1310720 | tf_op jit(solution)/shard_map/all_to_all | solution.py:26
  (12 shorter events, 1.8 us)
Async XLA Ops:
  27.7 14.0 %all-to-all-start.1 = ((f32[4,160,128]{2,1,0:T(8,128)}), f32[4,160,128]{2,1,0:T(8,128)S(1)}, u32[]{:S(2)}, u32[]{:S(2)}) async-start(f32[4,160,128]{2,1,0:T(8,128)} %get-tuple-element.15), calls=%async_computation.1 | async-start | bytes 655360 | tf_op jit(solution)/shard_map/all_to_all | solution.py:26
  31.2 25.0 %collective-permute-start = (f32[4,160,256]{2,1,0:T(8,128)S(1)}, f32[4,160,256]{2,1,0:T(8,128)S(1)}, u32[]{:S(2)}, u32[]{:S(2)}) collective-permute-start(f32[4,160,256]{2,1,0:T(8,128)S(1)} %all_to_all.45.row_head), channel_id=1, source_target_pairs={{0,128},{128,256},{256,384},{384,512},{512,640},{640,768},{768,896... | collective-permute-start | bytes 1966088 | tf_op jit(solution)/shard_map/ppermute | solution.py:22
  41.8 14.5 %collective-permute-start.1 = (f32[4,160,128]{2,1,0:T(8,128)S(1)}, f32[4,160,128]{2,1,0:T(8,128)S(1)}, u32[]{:S(2)}, u32[]{:S(2)}) collective-permute-start(f32[4,160,128]{2,1,0:T(8,128)S(1)} %all-to-all-done.1.row_tail), channel_id=1, source_target_pairs={{0,128},{128,256},{256,384},{384,512},{512,640},{640,768},{768,896... | collective-permute-start | bytes 983048 | tf_op jit(solution)/shard_map/ppermute | solution.py:22
  157.9 18.4 %collective-permute-start.2 = (f32[64,2,8,128]{3,2,1,0:T(8,128)S(1)}, f32[64,2,8,128]{3,2,1,0:T(8,128)S(1)}, u32[]{:S(2)}, u32[]{:S(2)}) collective-permute-start(f32[64,2,8,128]{3,2,1,0:T(8,128)S(1)} %slice.24), channel_id=1, source_target_pairs={{0,896},{128,0},{256,128},{384,256},{512,384},{640,512},{768,640},... | collective-permute-start | bytes 1572872 | tf_op jit(solution)/shard_map/ppermute | solution.py:22
  160.0 34.3 %collective-permute-start.3 = (f32[4,160,256]{2,1,0:T(8,128)S(1)}, f32[4,160,256]{2,1,0:T(8,128)}, u32[]{:S(2)}, u32[]{:S(2)}) collective-permute-start(f32[4,160,256]{2,1,0:T(8,128)S(1)} %all_to_all.45.row_head), channel_id=1, source_target_pairs={{0,896},{128,0},{256,128},{384,256},{512,384},{640,512},{768,640},... | collective-permute-start | bytes 1966088 | tf_op jit(solution)/shard_map/ppermute | solution.py:22
  176.2 18.1 %collective-permute-start.5 = (f32[64,2,8,128]{3,2,1,0:T(8,128)S(1)}, f32[64,2,8,128]{3,2,1,0:T(8,128)S(1)}, u32[]{:S(2)}, u32[]{:S(2)}) collective-permute-start(f32[64,2,8,128]{3,2,1,0:T(8,128)S(1)} %collective-permute-done.2.own_ref), channel_id=1, source_target_pairs={{0,1},{1,0},{2,3},{3,2},{4,5},{5,4},{6,7},{7,6},{8,9},{9,8},{10,11... | collective-permute-start | bytes 1572872 | tf_op jit(solution)/shard_map/ppermute | solution.py:239
  178.2 16.1 %collective-permute-start.4 = (f32[4,160,128]{2,1,0:T(8,128)S(1)}, f32[4,160,128]{2,1,0:T(8,128)S(1)}, u32[]{:S(2)}, u32[]{:S(2)}) collective-permute-start(f32[4,160,128]{2,1,0:T(8,128)S(1)} %all-to-all-done.1.row_tail), channel_id=1, source_target_pairs={{0,896},{128,0},{256,128},{384,256},{512,384},{640,512},{768,640},... | collective-permute-start | bytes 983048 | tf_op jit(solution)/shard_map/ppermute | solution.py:22

commit v6 on v4

--- a/solution.py
+++ b/solution.py
@@ -180,8 +180,8 @@
         out_ref[a] = row[bands * a : bands * (a + 1)] - 0.5 * fix[a]
 
 
-def above_kernel(core_ref, part_ref, above_head, above_tail, own_ref, partner_ref, out_ref):
-    first = core_ref[0] == 0
+def above_kernel(part_ref, above_head, above_tail, own_ref, partner_ref, out_ref):
+    first = lax.axis_index("c") == 0
     bands = part_ref.shape[1]
     above = halves(joined(above_head, above_tail))
 
@@ -208,7 +208,7 @@
     bands = orbitals.shape[0]
     points = orbitals.shape[1] * lax.axis_size(("z", "xl", "c"))
     members = lax.axis_size(RING)
-    head, tail = deal(orbitals)
+    head, tail = deal(pltpu.with_memory_space_constraint(orbitals, pltpu.HBM))
     head = exchange(head, "xh")
     below_head = passed_along(head, 1)
     tail = exchange(tail, "xh")
@@ -235,9 +235,8 @@
     corrected = pl.pallas_call(
         above_kernel,
         out_shape=jax.ShapeDtypeStruct(shape, jnp.float32),
-        in_specs=[pl.BlockSpec(memory_space=pltpu.SMEM)] + [pl.BlockSpec(memory_space=pltpu.VMEM)] * 5,
         compiler_params=pltpu.CompilerParams(vmem_limit_bytes=16 << 20),
-    )(lax.axis_index("c").reshape(1), part, above_head, above_tail, following, partner)
+    )(part, above_head, above_tail, following, partner)
     return collect(exchange(corrected, "xh"))
 
 

time: 229 us -> 228 us (level)
  no operation moved by 1% of the time
where the time goes in v6:
time: 228 us; the launch traced here: 227 us
  blocking collectives  166 us (73%)
  waiting for transfers between devices  28.7 us (13%)
  starting transfers between devices  21.4 us (9%)
  Pallas kernels  10.5 us (5%)
    all_to_all x7, blocking collectives, exchange(): return lax.all_to_all(pieces, axes, 0, 0)  166 us
    ppermute x5, waiting for transfers between devices, passed_along(): lax.ppermute(block, 'y', [(i, (i + distance) % count) for i in range(coun...  22.9 us
    ppermute x5, starting transfers between devices, passed_along(): lax.ppermute(block, 'y', [(i, (i + distance) % count) for i in range(coun...  16 us
    pallas_call x3, Pallas kernels, call(): pl.pallas_call(kernel, out_shape=jax.ShapeDtypeStruct(outs, jnp.float32),...  5.94 us
    all_to_all x1, waiting for transfers between devices, exchange(): return lax.all_to_all(pieces, axes, 0, 0)  5.76 us
  transfers between devices with their start and end apart: 7, of which 4 were waited for; matrix products, arithmetic and copies ran while one was open for 0% of the time, Pallas kernels for 2%

profile of v6, /device:TPU:48, one launch (start us, length us, event | category | flops | bytes accessed | tf_op | source)
XLA Modules:
  0.0 227.4 jit_solution(4332190022321194060)
XLA Ops:
  0.0 2.1 shard_map.17
  2.1 25.6 %all_to_all.40.row_head = f32[4,160,256]{2,1,0:T(8,128)S(1)} all-to-all(f32[4,160,256]{2,1,0:T(8,128)S(1)} %get-tuple-element.12), channel_id=1, replica_groups=mesh['y'=8,'xh'=4,'z'=8,'xl'=2,'c'=2] {'xh'}, dimensions={0} | all-to-all | bytes 1310720 | tf_op jit(solution)/shard_map/all_to_all | solution.py:26
  27.7 3.5 %all-to-all-start.1 = ((f32[4,160,128]{2,1,0:T(8,128)}), f32[4,160,128]{2,1,0:T(8,128)S(1)}, u32[]{:S(2)}, u32[]{:S(2)}) async-start(f32[4,160,128]{2,1,0:T(8,128)} %get-tuple-element.13), calls=%async_computation.1 | async-start | bytes 655360 | tf_op jit(solution)/shard_map/all_to_all | solution.py:26
  31.2 4.8 %collective-permute-start = (f32[4,160,256]{2,1,0:T(8,128)S(1)}, f32[4,160,256]{2,1,0:T(8,128)S(1)}, u32[]{:S(2)}, u32[]{:S(2)}) collective-permute-start(f32[4,160,256]{2,1,0:T(8,128)S(1)} %all_to_all.40.row_head), channel_id=1, source_target_pairs={{0,128},{128,256},{256,384},{384,512},{512,640},{640,768},{768,896... | collective-permute-start | bytes 1966088 | tf_op jit(solution)/shard_map/ppermute | solution.py:22
  36.0 5.8 %all-to-all-done.1.row_tail = f32[4,160,128]{2,1,0:T(8,128)S(1)} async-done(((f32[4,160,128]{2,1,0:T(8,128)}), f32[4,160,128]{2,1,0:T(8,128)S(1)}, u32[]{:S(2)}, u32[]{:S(2)}) %all-to-all-start.1) | async-done | bytes 327712 | tf_op jit(solution)/shard_map/all_to_all | solution.py:26
  41.8 4.8 %collective-permute-start.1 = (f32[4,160,128]{2,1,0:T(8,128)S(1)}, f32[4,160,128]{2,1,0:T(8,128)S(1)}, u32[]{:S(2)}, u32[]{:S(2)}) collective-permute-start(f32[4,160,128]{2,1,0:T(8,128)S(1)} %all-to-all-done.1.row_tail), channel_id=1, source_target_pairs={{0,128},{128,256},{256,384},{384,512},{512,640},{640,768},{768,896... | collective-permute-start | bytes 983048 | tf_op jit(solution)/shard_map/ppermute | solution.py:22
  46.6 1.5 shard_map.18
  48.1 4.6 %all_to_all.41 = f32[2,128,8,128]{3,2,1,0:T(8,128)S(1)} all-to-all(f32[2,128,8,128]{3,2,1,0:T(8,128)S(1)} %bitcast.5), channel_id=1, replica_groups=mesh['y'=8,'xh'=4,'z'=8,'xl'=2,'c'=2] {'c'}, dimensions={0} | all-to-all | bytes 2097152 | tf_op jit(solution)/shard_map/all_to_all | solution.py:26
  52.7 3.5 %collective-permute-done.1.refs_1_.below_tail = f32[4,160,128]{2,1,0:T(8,128)S(1)} collective-permute-done((f32[4,160,128]{2,1,0:T(8,128)S(1)}, f32[4,160,128]{2,1,0:T(8,128)S(1)}, u32[]{:S(2)}, u32[]{:S(2)}) %collective-permute-start.1) | collective-permute-done | bytes 327712 | tf_op jit(solution)/shard_map/ppermute | solution.py:22
  56.2 1.5 shard_map.19
  57.7 4.6 %all_to_all.42 = f32[2,128,8,128]{3,2,1,0:T(8,128)S(1)} all-to-all(f32[2,128,8,128]{3,2,1,0:T(8,128)S(1)} %bitcast.4), channel_id=1, replica_groups=mesh['y'=8,'xh'=4,'z'=8,'xl'=2,'c'=2] {'c'}, dimensions={0} | all-to-all | bytes 2097152 | tf_op jit(solution)/shard_map/all_to_all | solution.py:26
  62.5 59.5 %all_to_all.43 = f32[64,4,8,128]{3,2,1,0:T(8,128)S(1)} all-to-all(f32[64,4,8,128]{3,2,1,0:T(8,128)S(1)} %pad_maximum_fusion), channel_id=1, replica_groups=mesh['y'=8,'xh'=4,'z'=8,'xl'=2,'c'=2] {'xh','z','xl'}, dimensions={0} | all-to-all | bytes 2097152 | tf_op jit(solution)/shard_map/all_to_all | solution.py:26
  122.2 35.6 %all_to_all.44 = f32[64,4,8,128]{3,2,1,0:T(8,128)S(1)} all-to-all(f32[64,4,8,128]{3,2,1,0:T(8,128)S(1)} %broadcast_in_dim.4), channel_id=1, replica_groups=mesh['y'=8,'xh'=4,'z'=8,'xl'=2,'c'=2] {'xh','z','xl'}, dimensions={0} | all-to-all | bytes 2097152 | tf_op jit(solution)/shard_map/all_to_all | solution.py:26
  157.9 2.1 collective-permute-start.2
  160.0 2.4 %collective-permute-start.3 = (f32[4,160,256]{2,1,0:T(8,128)S(1)}, f32[4,160,256]{2,1,0:T(8,128)S(1)}, u32[]{:S(2)}, u32[]{:S(2)}) collective-permute-start(f32[4,160,256]{2,1,0:T(8,128)S(1)} %all_to_all.40.row_head), channel_id=1, source_target_pairs={{0,896},{128,0},{256,128},{384,256},{512,384},{640,512},{768,640},... | collective-permute-start | bytes 1966088 | tf_op jit(solution)/shard_map/ppermute | solution.py:22
  162.7 5.4 %all_to_all.45.units_ref = f32[2,64,4,8,128]{4,3,2,1,0:T(8,128)S(1)} all-to-all(f32[2,64,4,8,128]{4,3,2,1,0:T(8,128)S(1)} %broadcast_in_dim.5), channel_id=1, replica_groups=mesh['y'=8,'xh'=4,'z'=8,'xl'=2,'c'=2] {'c'}, dimensions={0} | all-to-all | bytes 4194304 | tf_op jit(solution)/shard_map/all_to_all | solution.py:26
  168.1 2.9 %shard_map.20.part_ref = f32[4,160,384]{2,1,0:T(8,128)S(1)} custom-call(f32[4,160,256]{2,1,0:T(8,128)S(1)} %all_to_all.40.row_head, f32[4,160,128]{2,1,0:T(8,128)S(1)} %all-to-all-done.1.row_tail, f32[4,160,256]{2,1,0:T(8,128)S(1)} %collective-permute-done.refs_0_.below_head, f32[4,160,128]{2,1,0:T(8,128)S(1)} %collective-permute-done.1.refs_1_.below_tail, ...), custom_call_target="tpu_custom_call" | custom-call | tf_op jit(solution)/shard_map/pallas_call | solution.py:51
  171.1 5.2 %collective-permute-done.2.own_ref = f32[64,2,8,128]{3,2,1,0:T(8,128)S(1)} collective-permute-done((f32[64,2,8,128]{3,2,1,0:T(8,128)S(1)}, f32[64,2,8,128]{3,2,1,0:T(8,128)S(1)}, u32[]{:S(2)}, u32[]{:S(2)}) %collective-permute-start.2) | collective-permute-done | bytes 524320 | tf_op jit(solution)/shard_map/ppermute | solution.py:22
  176.2 1.9 collective-permute-start.5
  178.2 1.9 collective-permute-start.4
  180.1 14.2 %collective-permute-done.4.above_tail = f32[4,160,128]{2,1,0:T(8,128)S(1)} collective-permute-done((f32[4,160,128]{2,1,0:T(8,128)S(1)}, f32[4,160,128]{2,1,0:T(8,128)S(1)}, u32[]{:S(2)}, u32[]{:S(2)}) %collective-permute-start.4) | collective-permute-done | bytes 327712 | tf_op jit(solution)/shard_map/ppermute | solution.py:22
  194.3 1.5 shard_map.21
  195.8 30.6 %all_to_all.46.quarters = f32[4,160,384]{2,1,0:T(8,128)S(1)} all-to-all(f32[4,160,384]{2,1,0:T(8,128)S(1)} %shard_map.21), channel_id=1, replica_groups=mesh['y'=8,'xh'=4,'z'=8,'xl'=2,'c'=2] {'xh'}, dimensions={0} | all-to-all | bytes 1966080 | tf_op jit(solution)/shard_map/all_to_all | solution.py:26
  226.4 1.0 shard_map.22
  (11 shorter events, 0.8 us)
Async XLA Ops:
  27.7 14.0 %all-to-all-start.1 = ((f32[4,160,128]{2,1,0:T(8,128)}), f32[4,160,128]{2,1,0:T(8,128)S(1)}, u32[]{:S(2)}, u32[]{:S(2)}) async-start(f32[4,160,128]{2,1,0:T(8,128)} %get-tuple-element.13), calls=%async_computation.1 | async-start | bytes 655360 | tf_op jit(solution)/shard_map/all_to_all | solution.py:26
  31.2 25.0 %collective-permute-start = (f32[4,160,256]{2,1,0:T(8,128)S(1)}, f32[4,160,256]{2,1,0:T(8,128)S(1)}, u32[]{:S(2)}, u32[]{:S(2)}) collective-permute-start(f32[4,160,256]{2,1,0:T(8,128)S(1)} %all_to_all.40.row_head), channel_id=1, source_target_pairs={{0,128},{128,256},{256,384},{384,512},{512,640},{640,768},{768,896... | collective-permute-start | bytes 1966088 | tf_op jit(solution)/shard_map/ppermute | solution.py:22
  41.8 14.5 %collective-permute-start.1 = (f32[4,160,128]{2,1,0:T(8,128)S(1)}, f32[4,160,128]{2,1,0:T(8,128)S(1)}, u32[]{:S(2)}, u32[]{:S(2)}) collective-permute-start(f32[4,160,128]{2,1,0:T(8,128)S(1)} %all-to-all-done.1.row_tail), channel_id=1, source_target_pairs={{0,128},{128,256},{256,384},{384,512},{512,640},{640,768},{768,896... | collective-permute-start | bytes 983048 | tf_op jit(solution)/shard_map/ppermute | solution.py:22
  157.9 18.4 %collective-permute-start.2 = (f32[64,2,8,128]{3,2,1,0:T(8,128)S(1)}, f32[64,2,8,128]{3,2,1,0:T(8,128)S(1)}, u32[]{:S(2)}, u32[]{:S(2)}) collective-permute-start(f32[64,2,8,128]{3,2,1,0:T(8,128)S(1)} %slice.24), channel_id=1, source_target_pairs={{0,896},{128,0},{256,128},{384,256},{512,384},{640,512},{768,640},... | collective-permute-start | bytes 1572872 | tf_op jit(solution)/shard_map/ppermute | solution.py:22
  160.0 34.3 %collective-permute-start.3 = (f32[4,160,256]{2,1,0:T(8,128)S(1)}, f32[4,160,256]{2,1,0:T(8,128)S(1)}, u32[]{:S(2)}, u32[]{:S(2)}) collective-permute-start(f32[4,160,256]{2,1,0:T(8,128)S(1)} %all_to_all.40.row_head), channel_id=1, source_target_pairs={{0,896},{128,0},{256,128},{384,256},{512,384},{640,512},{768,640},... | collective-permute-start | bytes 1966088 | tf_op jit(solution)/shard_map/ppermute | solution.py:22
  176.2 18.1 %collective-permute-start.5 = (f32[64,2,8,128]{3,2,1,0:T(8,128)S(1)}, f32[64,2,8,128]{3,2,1,0:T(8,128)S(1)}, u32[]{:S(2)}, u32[]{:S(2)}) collective-permute-start(f32[64,2,8,128]{3,2,1,0:T(8,128)S(1)} %collective-permute-done.2.own_ref), channel_id=1, source_target_pairs={{0,1},{1,0},{2,3},{3,2},{4,5},{5,4},{6,7},{7,6},{8,9},{9,8},{10,11... | collective-permute-start | bytes 1572872 | tf_op jit(solution)/shard_map/ppermute | solution.py:234
  178.2 16.1 %collective-permute-start.4 = (f32[4,160,128]{2,1,0:T(8,128)S(1)}, f32[4,160,128]{2,1,0:T(8,128)S(1)}, u32[]{:S(2)}, u32[]{:S(2)}) collective-permute-start(f32[4,160,128]{2,1,0:T(8,128)S(1)} %all-to-all-done.1.row_tail), channel_id=1, source_target_pairs={{0,896},{128,0},{256,128},{384,256},{512,384},{640,512},{768,640},... | collective-permute-start | bytes 983048 | tf_op jit(solution)/shard_map/ppermute | solution.py:22

commit v7 on v6

--- a/solution.py
+++ b/solution.py
@@ -200,6 +200,15 @@
         out_ref[a] = part_ref[a] - 0.5 * fix[a]
 
 
+def sums_kernel(inner_ref, outer_ref, out_ref):
+    out_ref[:, :2] = inner_ref[0] + inner_ref[1]
+    out_ref[:, 2:] = outer_ref[0] + outer_ref[1]
+
+
+def share_kernel(points, parts_ref, out_ref):
+    out_ref[...] = jnp.broadcast_to((parts_ref[...].sum(0) / points)[None], out_ref.shape)
+
+
 INNER = [(3, 0, 4), (2, 0, 3), (1, 0, 2), (0, 0, 1)]
 OUTER = [(0, 0, 4), (1, 1, 4), (2, 2, 4), (3, 3, 4)]
 
@@ -219,14 +228,14 @@
     def tiles(order, *operands):
         units = call(functools.partial(tiles_kernel, order), (UNITS, ROWS, UNIT), *operands)
         pair = exchange(units.reshape(2, UNITS // 2, ROWS, UNIT), "c")
-        return (pair[0] + pair[1]).reshape(members, -1, ROWS, UNIT)
+        return pair.reshape(2, members, -1, ROWS, UNIT)
 
     inner = tiles(INNER, head, tail)
     below_head, below_tail, inner = lax.optimization_barrier((below_head, below_tail, inner))
     outer = tiles(OUTER, head, tail, below_head, below_tail)
-    share = exchange(jnp.concatenate([inner, outer], 1), RING)
-    share = share.sum(0) / points
-    both = spread(share, RING)
+    parts = exchange(call(sums_kernel, (members, 4, ROWS, UNIT), inner, outer), RING)
+    shares = call(functools.partial(share_kernel, points), parts.shape, parts)
+    both = exchange(shares, RING)
     following = passed_along(both[:, 2:], -1)
     shape = (GROUPS, bands, orbitals.shape[1] // GROUPS)
     part = call(apply_kernel, shape, head, tail, below_head, below_tail, spread(both, "c"))

time: 228 us -> 228 us (level)
  blocking collectives: 166 us -> 161 us
  starting transfers between devices: 21.4 us -> 25 us
    all_to_all x7 -> x6, blocking collectives: 166 us -> 161 us  [exchange(): return lax.all_to_all(pieces, axes, 0, 0)]
    all_to_all x1 -> x2, starting transfers between devices: 3.45 us -> 7.03 us  [exchange(): return lax.all_to_all(pieces, axes, 0, 0)]
    pallas_call x3 -> x5, Pallas kernels: 5.94 us -> 7.2 us  [call(): pl.pallas_call(kernel, out_shape=jax.ShapeDtypeStruct(outs, jnp.float32),...]
    all_to_all x1 -> x2, waiting for transfers between devices: 5.76 us -> 5.76 us  [exchange(): return lax.all_to_all(pieces, axes, 0, 0)]
  transfers between devices with their start and end apart: 7 -> 8, of which waited for: 4 -> 4; matrix products, arithmetic and copies ran while one was open for 0% -> 0% of each run, Pallas kernels for 2% -> 2%
where the time goes in v7:
time: 228 us; the launch traced here: 227 us
  blocking collectives  161 us (71%)
  waiting for transfers between devices  28.8 us (13%)
  starting transfers between devices  25 us (11%)
  Pallas kernels  11.8 us (5%)
    all_to_all x6, blocking collectives, exchange(): return lax.all_to_all(pieces, axes, 0, 0)  161 us
    ppermute x5, waiting for transfers between devices, passed_along(): lax.ppermute(block, 'y', [(i, (i + distance) % count) for i in range(coun...  23 us
    ppermute x5, starting transfers between devices, passed_along(): lax.ppermute(block, 'y', [(i, (i + distance) % count) for i in range(coun...  16 us
    pallas_call x5, Pallas kernels, call(): pl.pallas_call(kernel, out_shape=jax.ShapeDtypeStruct(outs, jnp.float32),...  7.2 us
    all_to_all x2, starting transfers between devices, exchange(): return lax.all_to_all(pieces, axes, 0, 0)  7.03 us
    all_to_all x2, waiting for transfers between devices, exchange(): return lax.all_to_all(pieces, axes, 0, 0)  5.76 us
  transfers between devices with their start and end apart: 8, of which 4 were waited for; matrix products, arithmetic and copies ran while one was open for 0% of the time, Pallas kernels for 2%

profile of v7, /device:TPU:48, one launch (start us, length us, event | category | flops | bytes accessed | tf_op | source)
XLA Modules:
  0.0 227.3 jit_solution(13005486929780223856)
XLA Ops:
  0.0 2.1 shard_map.17
  2.1 25.6 %all_to_all.40.row_head = f32[4,160,256]{2,1,0:T(8,128)S(1)} all-to-all(f32[4,160,256]{2,1,0:T(8,128)S(1)} %get-tuple-element.12), channel_id=1, replica_groups=mesh['y'=8,'xh'=4,'z'=8,'xl'=2,'c'=2] {'xh'}, dimensions={0} | all-to-all | bytes 1310720 | tf_op jit(solution)/shard_map/all_to_all | solution.py:26
  27.7 3.5 %all-to-all-start.1 = ((f32[4,160,128]{2,1,0:T(8,128)}), f32[4,160,128]{2,1,0:T(8,128)S(1)}, u32[]{:S(2)}, u32[]{:S(2)}) async-start(f32[4,160,128]{2,1,0:T(8,128)} %get-tuple-element.13), calls=%async_computation.1 | async-start | bytes 655360 | tf_op jit(solution)/shard_map/all_to_all | solution.py:26
  31.2 4.8 %collective-permute-start = (f32[4,160,256]{2,1,0:T(8,128)S(1)}, f32[4,160,256]{2,1,0:T(8,128)S(1)}, u32[]{:S(2)}, u32[]{:S(2)}) collective-permute-start(f32[4,160,256]{2,1,0:T(8,128)S(1)} %all_to_all.40.row_head), channel_id=1, source_target_pairs={{0,128},{128,256},{256,384},{384,512},{512,640},{640,768},{768,896... | collective-permute-start | bytes 1966088 | tf_op jit(solution)/shard_map/ppermute | solution.py:22
  36.0 5.8 %all-to-all-done.1.row_tail = f32[4,160,128]{2,1,0:T(8,128)S(1)} async-done(((f32[4,160,128]{2,1,0:T(8,128)}), f32[4,160,128]{2,1,0:T(8,128)S(1)}, u32[]{:S(2)}, u32[]{:S(2)}) %all-to-all-start.1) | async-done | bytes 327712 | tf_op jit(solution)/shard_map/all_to_all | solution.py:26
  41.8 4.8 %collective-permute-start.1 = (f32[4,160,128]{2,1,0:T(8,128)S(1)}, f32[4,160,128]{2,1,0:T(8,128)S(1)}, u32[]{:S(2)}, u32[]{:S(2)}) collective-permute-start(f32[4,160,128]{2,1,0:T(8,128)S(1)} %all-to-all-done.1.row_tail), channel_id=1, source_target_pairs={{0,128},{128,256},{256,384},{384,512},{512,640},{640,768},{768,896... | collective-permute-start | bytes 983048 | tf_op jit(solution)/shard_map/ppermute | solution.py:22
  46.6 2.5 %shard_map.18 = f32[256,8,128]{2,1,0:T(8,128)} custom-call(f32[4,160,256]{2,1,0:T(8,128)S(1)} %all_to_all.40.row_head, f32[4,160,128]{2,1,0:T(8,128)S(1)} %all-to-all-done.1.row_tail), custom_call_target="tpu_custom_call" | custom-call | tf_op jit(solution)/shard_map/pallas_call | solution.py:51
  49.1 3.6 %all-to-all-start.2 = ((f32[2,128,8,128]{3,2,1,0:T(8,128)}), f32[2,128,8,128]{3,2,1,0:T(8,128)S(1)}, u32[]{:S(2)}, u32[]{:S(2)}) async-start(f32[2,128,8,128]{3,2,1,0:T(8,128)} %bitcast), calls=%async_computation.2 | async-start | bytes 2097152 | tf_op jit(solution)/shard_map/all_to_all | solution.py:26
  52.6 3.6 %collective-permute-done.1.refs_1_.below_tail = f32[4,160,128]{2,1,0:T(8,128)S(1)} collective-permute-done((f32[4,160,128]{2,1,0:T(8,128)S(1)}, f32[4,160,128]{2,1,0:T(8,128)S(1)}, u32[]{:S(2)}, u32[]{:S(2)}) %collective-permute-start.1) | collective-permute-done | bytes 327712 | tf_op jit(solution)/shard_map/ppermute | solution.py:22
  56.2 1.5 shard_map.19
  57.7 4.6 %all_to_all.41 = f32[2,128,8,128]{3,2,1,0:T(8,128)S(1)} all-to-all(f32[2,128,8,128]{3,2,1,0:T(8,128)S(1)} %bitcast.6), channel_id=1, replica_groups=mesh['y'=8,'xh'=4,'z'=8,'xl'=2,'c'=2] {'c'}, dimensions={0} | all-to-all | bytes 2097152 | tf_op jit(solution)/shard_map/all_to_all | solution.py:26
  62.4 59.5 %all_to_all.42.parts_ref = f32[64,4,8,128]{3,2,1,0:T(8,128)S(1)} all-to-all(f32[64,4,8,128]{3,2,1,0:T(8,128)S(1)} %shard_map.20), channel_id=1, replica_groups=mesh['y'=8,'xh'=4,'z'=8,'xl'=2,'c'=2] {'xh','z','xl'}, dimensions={0} | all-to-all | bytes 2097152 | tf_op jit(solution)/shard_map/all_to_all | solution.py:26
  122.1 35.6 %all_to_all.43 = f32[64,4,8,128]{3,2,1,0:T(8,128)S(1)} all-to-all(f32[64,4,8,128]{3,2,1,0:T(8,128)S(1)} %shard_map.21), channel_id=1, replica_groups=mesh['y'=8,'xh'=4,'z'=8,'xl'=2,'c'=2] {'xh','z','xl'}, dimensions={0} | all-to-all | bytes 2097152 | tf_op jit(solution)/shard_map/all_to_all | solution.py:26
  157.8 2.1 collective-permute-start.2
  159.9 2.4 %collective-permute-start.3 = (f32[4,160,256]{2,1,0:T(8,128)S(1)}, f32[4,160,256]{2,1,0:T(8,128)S(1)}, u32[]{:S(2)}, u32[]{:S(2)}) collective-permute-start(f32[4,160,256]{2,1,0:T(8,128)S(1)} %all_to_all.40.row_head), channel_id=1, source_target_pairs={{0,896},{128,0},{256,128},{384,256},{512,384},{640,512},{768,640},... | collective-permute-start | bytes 1966088 | tf_op jit(solution)/shard_map/ppermute | solution.py:22
  162.6 5.4 %all_to_all.44.units_ref = f32[2,64,4,8,128]{4,3,2,1,0:T(8,128)S(1)} all-to-all(f32[2,64,4,8,128]{4,3,2,1,0:T(8,128)S(1)} %broadcast_in_dim.2), channel_id=1, replica_groups=mesh['y'=8,'xh'=4,'z'=8,'xl'=2,'c'=2] {'c'}, dimensions={0} | all-to-all | bytes 4194304 | tf_op jit(solution)/shard_map/all_to_all | solution.py:26
  168.0 2.9 %shard_map.22.part_ref = f32[4,160,384]{2,1,0:T(8,128)S(1)} custom-call(f32[4,160,256]{2,1,0:T(8,128)S(1)} %all_to_all.40.row_head, f32[4,160,128]{2,1,0:T(8,128)S(1)} %all-to-all-done.1.row_tail, f32[4,160,256]{2,1,0:T(8,128)S(1)} %collective-permute-done.refs_0_.below_head, f32[4,160,128]{2,1,0:T(8,128)S(1)} %collective-permute-done.1.refs_1_.below_tail, ...), custom_call_target="tpu_custom_call" | custom-call | tf_op jit(solution)/shard_map/pallas_call | solution.py:51
  170.9 5.2 %collective-permute-done.2.own_ref = f32[64,2,8,128]{3,2,1,0:T(8,128)S(1)} collective-permute-done((f32[64,2,8,128]{3,2,1,0:T(8,128)S(1)}, f32[64,2,8,128]{3,2,1,0:T(8,128)S(1)}, u32[]{:S(2)}, u32[]{:S(2)}) %collective-permute-start.2) | collective-permute-done | bytes 524320 | tf_op jit(solution)/shard_map/ppermute | solution.py:22
  176.1 1.9 collective-permute-start.5
  178.0 1.9 collective-permute-start.4
  180.0 14.2 %collective-permute-done.4.above_tail = f32[4,160,128]{2,1,0:T(8,128)S(1)} collective-permute-done((f32[4,160,128]{2,1,0:T(8,128)S(1)}, f32[4,160,128]{2,1,0:T(8,128)S(1)}, u32[]{:S(2)}, u32[]{:S(2)}) %collective-permute-start.4) | collective-permute-done | bytes 327712 | tf_op jit(solution)/shard_map/ppermute | solution.py:22
  194.2 1.5 shard_map.23
  195.7 30.6 %all_to_all.45.quarters = f32[4,160,384]{2,1,0:T(8,128)S(1)} all-to-all(f32[4,160,384]{2,1,0:T(8,128)S(1)} %shard_map.23), channel_id=1, replica_groups=mesh['y'=8,'xh'=4,'z'=8,'xl'=2,'c'=2] {'xh'}, dimensions={0} | all-to-all | bytes 1966080 | tf_op jit(solution)/shard_map/all_to_all | solution.py:26
  226.3 1.0 shard_map.24
  (8 shorter events, 0.6 us)
Async XLA Ops:
  27.7 14.0 %all-to-all-start.1 = ((f32[4,160,128]{2,1,0:T(8,128)}), f32[4,160,128]{2,1,0:T(8,128)S(1)}, u32[]{:S(2)}, u32[]{:S(2)}) async-start(f32[4,160,128]{2,1,0:T(8,128)} %get-tuple-element.13), calls=%async_computation.1 | async-start | bytes 655360 | tf_op jit(solution)/shard_map/all_to_all | solution.py:26
  31.2 25.0 %collective-permute-start = (f32[4,160,256]{2,1,0:T(8,128)S(1)}, f32[4,160,256]{2,1,0:T(8,128)S(1)}, u32[]{:S(2)}, u32[]{:S(2)}) collective-permute-start(f32[4,160,256]{2,1,0:T(8,128)S(1)} %all_to_all.40.row_head), channel_id=1, source_target_pairs={{0,128},{128,256},{256,384},{384,512},{512,640},{640,768},{768,896... | collective-permute-start | bytes 1966088 | tf_op jit(solution)/shard_map/ppermute | solution.py:22
  41.8 14.5 %collective-permute-start.1 = (f32[4,160,128]{2,1,0:T(8,128)S(1)}, f32[4,160,128]{2,1,0:T(8,128)S(1)}, u32[]{:S(2)}, u32[]{:S(2)}) collective-permute-start(f32[4,160,128]{2,1,0:T(8,128)S(1)} %all-to-all-done.1.row_tail), channel_id=1, source_target_pairs={{0,128},{128,256},{256,384},{384,512},{512,640},{640,768},{768,896... | collective-permute-start | bytes 983048 | tf_op jit(solution)/shard_map/ppermute | solution.py:22
  49.1 7.2 %all-to-all-start.2 = ((f32[2,128,8,128]{3,2,1,0:T(8,128)}), f32[2,128,8,128]{3,2,1,0:T(8,128)S(1)}, u32[]{:S(2)}, u32[]{:S(2)}) async-start(f32[2,128,8,128]{3,2,1,0:T(8,128)} %bitcast), calls=%async_computation.2 | async-start | bytes 2097152 | tf_op jit(solution)/shard_map/all_to_all | solution.py:26
  157.8 18.4 %collective-permute-start.2 = (f32[64,2,8,128]{3,2,1,0:T(8,128)S(1)}, f32[64,2,8,128]{3,2,1,0:T(8,128)S(1)}, u32[]{:S(2)}, u32[]{:S(2)}) collective-permute-start(f32[64,2,8,128]{3,2,1,0:T(8,128)S(1)} %slice.4), channel_id=1, source_target_pairs={{0,896},{128,0},{256,128},{384,256},{512,384},{640,512},{768,640},... | collective-permute-start | bytes 1572872 | tf_op jit(solution)/shard_map/ppermute | solution.py:22
  159.9 34.3 %collective-permute-start.3 = (f32[4,160,256]{2,1,0:T(8,128)S(1)}, f32[4,160,256]{2,1,0:T(8,128)S(1)}, u32[]{:S(2)}, u32[]{:S(2)}) collective-permute-start(f32[4,160,256]{2,1,0:T(8,128)S(1)} %all_to_all.40.row_head), channel_id=1, source_target_pairs={{0,896},{128,0},{256,128},{384,256},{512,384},{640,512},{768,640},... | collective-permute-start | bytes 1966088 | tf_op jit(solution)/shard_map/ppermute | solution.py:22
  176.1 18.1 %collective-permute-start.5 = (f32[64,2,8,128]{3,2,1,0:T(8,128)S(1)}, f32[64,2,8,128]{3,2,1,0:T(8,128)S(1)}, u32[]{:S(2)}, u32[]{:S(2)}) collective-permute-start(f32[64,2,8,128]{3,2,1,0:T(8,128)S(1)} %collective-permute-done.2.own_ref), channel_id=1, source_target_pairs={{0,1},{1,0},{2,3},{3,2},{4,5},{5,4},{6,7},{7,6},{8,9},{9,8},{10,11... | collective-permute-start | bytes 1572872 | tf_op jit(solution)/shard_map/ppermute | solution.py:243
  178.0 16.1 %collective-permute-start.4 = (f32[4,160,128]{2,1,0:T(8,128)S(1)}, f32[4,160,128]{2,1,0:T(8,128)S(1)}, u32[]{:S(2)}, u32[]{:S(2)}) collective-permute-start(f32[4,160,128]{2,1,0:T(8,128)S(1)} %all-to-all-done.1.row_tail), channel_id=1, source_target_pairs={{0,896},{128,0},{256,128},{384,256},{512,384},{640,512},{768,640},... | collective-permute-start | bytes 983048 | tf_op jit(solution)/shard_map/ppermute | solution.py:22
